TPU v7x, 256 devices: a whole 4x4x8 slice. The times are simulated.
256 devices in a mesh: seq: 64 (over y, z, core), pool: 4 (over x).
Axes of the slice: x: 4, y: 4, z: 8, core: 2. Of those that a mesh axis runs over, the one named last changes fastest.
Arguments:
- query_rows: bfloat16 [32768, 4096], P('seq', 'pool'), may hold values from -6 to 6
- key_rows: bfloat16 [32768, 4096], P('seq', 'pool'), may hold values from -6 to 6
- value_rows: bfloat16 [32768, 4096], P('seq', 'pool'), may hold values from -6 to 6
- log_decay: float32 [32, 32768], P('pool', 'seq'), may hold values from -0.7 to 0
- residual: bfloat16 [32768, 4096], P(('seq', 'pool')), may hold values from -6 to 6
- out_weight: bfloat16 [4096, 4096], P('pool', 'seq'), may hold values from -0.09375 to 0.09375
- norm_gain: float32 [4096], replicated, may hold values from 0.5 to 1.5
- kv_weight: bfloat16 [4096, 1024], P('seq'), may hold values from -0.09375 to 0.09375
- block_table: int32 [256, 2], P(('seq', 'pool')), may hold values from 0 to 3, as said below
Outputs:
- page_cache: bfloat16 [64, 4, 2, 128, 1024], P('seq', 'pool')
Inputs may be any that keep to these rules, and one draw needn't show every extreme that they name: `block_table`: column 0 is a page's pool device, column 1 its slot there. The pages of one index of seq go to pool devices of that same index, no two to the same device and slot; one pool device receives exactly 2 of them, each other at most 2, and all 1 pages of some device go to that one.
All inputs are finite; a program needn't handle non-finite values.
Results may differ from a plain program's by a relative error of at most 0.0056.
Values may be sent and summed in bfloat16 or wider, within the bound.
A program may use at most 128 MiB of HBM per device.

v0:
```python
import jax
import jax.numpy as jnp
from jax import lax
from jax.sharding import PartitionSpec as P

HD = 128
PAGE = 128
BLK = 512


def entering(part, axis, combine, identity):
    place = lax.axis_index(axis)
    gathered = jax.tree.map(lambda a: lax.all_gather(a, axis), part)
    state = jax.tree.map(lambda a, e: jnp.zeros_like(a) + jnp.asarray(e, a.dtype), part, identity)

    def one(hop, state):
        return combine(
            state, jax.tree.map(lambda a: lax.dynamic_index_in_dim(a, hop, 0, False), gathered)
        )

    return lax.fori_loop(0, place, one, state)


def head_major(matrix, head_count):
    return matrix.reshape(BLK, head_count, HD).transpose(1, 0, 2)


def combine_states(earlier, later):
    return (earlier[0] + later[0], jnp.exp(later[0])[:, None, None] * earlier[1] + later[1])


def on_device(
    query_rows,
    key_rows,
    value_rows,
    log_decay,
    residual,
    out_weight,
    norm_gain,
    kv_weight,
    block_table,
):
    head_count = query_rows.shape[1] // HD
    lower_mask = jnp.tril(jnp.ones((BLK, BLK), dtype=bool))
    query_blk = head_major(query_rows, head_count)
    key_blk = head_major(key_rows, head_count)
    value_blk = head_major(value_rows, head_count)
    cumulative = jnp.cumsum(log_decay, axis=1)
    block_total = cumulative[:, -1]
    log_gap = jnp.where(lower_mask[None], cumulative[:, :, None] - cumulative[:, None, :], 0.0)
    products = jnp.einsum("hid,hjd->hij", query_blk, key_blk, preferred_element_type=jnp.float32)
    scores = jnp.where(lower_mask[None], products * jnp.exp(log_gap), 0.0).astype(jnp.bfloat16)
    inner = jnp.einsum("hij,hjd->hid", scores, value_blk, preferred_element_type=jnp.float32)
    weighted = (
        key_blk.astype(jnp.float32) * jnp.exp(block_total[:, None] - cumulative)[:, :, None]
    ).astype(jnp.bfloat16)
    update = jnp.einsum("hjd,hje->hde", weighted, value_blk, preferred_element_type=jnp.float32)
    query_list = [query_blk]
    inner_list = [inner]
    update_list = [update]
    cumul_list = [cumulative]
    total_list = [block_total]
    state_sum = jnp.zeros((head_count, HD, HD), jnp.float32)
    block_index = 0
    state_sum = (
        jnp.exp(total_list[block_index])[:, None, None] * state_sum + update_list[block_index]
    )
    log_sum = total_list[block_index]
    incoming = entering(
        (log_sum, state_sum),
        "seq",
        combine_states,
        (jnp.zeros_like(log_sum), jnp.zeros_like(state_sum)),
    )
    carried = incoming[1]
    block_index = 0
    outer = (
        jnp.einsum(
            "hid,hde->hie",
            query_list[block_index].astype(jnp.float32),
            carried,
            precision=lax.Precision.HIGHEST,
        )
        * jnp.exp(cumul_list[block_index])[:, :, None]
    )
    retained = inner_list[block_index] + outer
    scaled = retained * lax.rsqrt(jnp.mean(retained * retained, axis=-1, keepdims=True) + 1e-05)
    mixed_list = scaled.transpose(1, 0, 2).reshape(BLK, head_count * HD).astype(jnp.bfloat16)
    partial_value = jnp.dot(
        mixed_list,
        lax.all_gather(out_weight, "seq", axis=1, tiled=True),
        preferred_element_type=jnp.float32,
    )
    summed = lax.psum_scatter(partial_value, "pool", scatter_dimension=0, tiled=True)
    hidden = residual.astype(jnp.float32) + summed
    normed = (
        hidden * lax.rsqrt(jnp.mean(hidden * hidden, axis=-1, keepdims=True) + 1e-05) * norm_gain
    ).astype(jnp.bfloat16)
    pool_count = lax.axis_size("pool")
    pages_here = block_table.shape[0]
    slot_count = 2 * pages_here
    cache_width = kv_weight.shape[1]
    owner_ids = jnp.arange(pool_count, dtype=jnp.int32)
    slot_ids = jnp.arange(slot_count, dtype=jnp.int32)
    owner_match = block_table[:, 0][:, None] == owner_ids[None, :]
    slot_match = block_table[:, 1][:, None] == slot_ids[None, :]
    placed = jnp.logical_and(owner_match[:, :, None], slot_match[:, None, :]).astype(jnp.bfloat16)
    cache_rows = jnp.dot(
        normed,
        lax.all_gather(kv_weight, "seq", axis=0, tiled=True),
        preferred_element_type=jnp.float32,
    ).astype(jnp.bfloat16)
    own_pages = cache_rows.reshape(pages_here, PAGE, cache_width)
    outgoing = jnp.where(
        owner_match.T[:, :, None, None], own_pages[None], jnp.zeros((), jnp.bfloat16)
    )
    slot_tags = placed.transpose(1, 0, 2)
    arrived, arrived_tags = (
        lax.all_to_all(outgoing, "pool", split_axis=0, concat_axis=0, tiled=True),
        lax.all_to_all(slot_tags, "pool", split_axis=0, concat_axis=0, tiled=True),
    )
    page_cache = jnp.einsum(
        "ips,ipqc->sqc", arrived_tags, arrived, preferred_element_type=jnp.float32
    ).astype(jnp.bfloat16)
    return page_cache.reshape(1, 1, slot_count, PAGE, cache_width)


def solution(mesh):
    placed = (
        P("seq", "pool"),
        P("seq", "pool"),
        P("seq", "pool"),
        P("pool", "seq"),
        P(("seq", "pool"), None),
        P("pool", "seq"),
        P(),
        P("seq", None),
        P(("seq", "pool"), None),
    )
    return jax.shard_map(
        on_device,
        mesh=mesh,
        in_specs=placed,
        out_specs=P("seq", "pool", None, None, None),
        check_vma=False,
    )
```

profile of v0, /device:TPU:6, one launch (start us, length us, event | category | flops | bytes accessed | tf_op | source)
XLA Modules:
  0.0 454.0 jit_solution(11323797303742219468)
XLA Ops:
  6.5 0.0 copy-start
  6.5 2.4 reduce-window.6
  8.9 0.2 slice_reduce_fusion
  9.1 0.1 exponential_bitcast_fusion.1
  9.2 0.2 slice_reduce_fusion.1
  9.4 0.1 fusion.23
  9.5 1.5 copy.46
  11.0 0.0 copy-start.9
  11.0 0.0 copy-done.5
  11.0 1.3 convolution_add_fusion
  12.3 0.0 all-gather.10.cloned.1.call-update
  12.3 0.0 all-gather.6.cloned.1.call-start
  12.3 0.7 all-gather.6.cloned.1.call-update
  13.1 0.0 reduce-scatter.2.cloned.1.call-start
  13.1 0.6 dynamic-slice
  14.4 0.2 dynamic-update-slice
  14.6 136.1 %all-reduce = f32[512]{0:T(512)S(1)} all-reduce(f32[512]{0:T(512)S(1)} %dynamic-update-slice), channel_id=2, replica_groups=mesh['seq'=64,'pool'=4] {'seq'}, use_global_device_ids=true, to_apply=%add | all-reduce | flops 512 | bytes 4096
  150.7 0.1 reshape.211
  150.8 1.3 copy.51
  152.1 0.1 iota_compare_fusion
  152.2 5.2 %all-gather.10.cloned.1.call-done = f32[512,128,128]{2,1,0:T(8,128)} async-done(((f32[8,128,128]{2,1,0:T(8,128)}), f32[512,128,128]{2,1,0:T(8,128)}) %all-gather.10.cloned.1.call-update) | async-done | bytes 33554448 | tf_op jit(solution)/shard_map/all_gather | solution.py:13
  157.5 2.4 fusion.11
  159.9 7.4 %fusion.5 = (f32[8,512]{1,0:T(8,128)S(1)}, f32[8,512,128]{1,2,0:T(8,128)}) fusion(f32[8,128,512]{2,1,0:T(8,128)} %fusion.11, f32[8,512]{1,0:T(8,128)S(1)} %get-tuple-element.62, bf16[8,512,128]{2,0,1:T(8,128)(2,1)} %bitcast.94, f32[8,512]{1,0:T(8,128)S(1)} %get-tuple-element.61, pred[512,512]{1,0:T(8,128)(4,1)S(1)} %iota_compare_fusion, ...), kind=kOutput, calls=%fused_computation.8 | convolution fusion | flops 1086320640 | bytes 7651328 | tf_op jit(solution)/shard_map/hij,hjd->hid/dot_general | solution.py:53
  167.3 2.2 fusion.8
  169.5 70.6 %all-gather.6.cloned.1.call-done = bf16[1024,4096]{0,1:T(8,128)(2,1)} async-done(((bf16[1024,64]{0,1:T(8,128)(2,1)}), bf16[1024,4096]{0,1:T(8,128)(2,1)}) %all-gather.6.cloned.1.call-update) | async-done | bytes 8388624 | tf_op jit(solution)/shard_map/all_gather | solution.py:91
  240.1 10.3 %fusion.25 = f32[512,4096]{1,0:T(8,128)} fusion(bf16[512,1024]{0,1:T(8,128)(2,1)S(1)} %bitcast.90, bf16[1024,4096]{0,1:T(8,128)(2,1)} %all-gather.6.cloned.1.call-done), kind=kOutput, calls=%fused_computation.50 | convolution fusion | flops 4294967296 | bytes 17825792 | tf_op jit(solution)/shard_map/dot_general | solution.py:89
  250.4 0.0 reduce-scatter.2.cloned.1.call-update
  250.4 0.0 copy-start.7
  250.4 0.0 all-gather.8.cloned.1.call-start
  250.5 0.5 all-gather.8.cloned.1.call-update
  251.0 0.0 copy-done.8
  251.1 0.6 fusion.24
  251.6 0.7 iota_compare_fusion.2
  252.3 0.7 iota_compare_fusion.1
  253.0 0.7 and_convert_fusion
  253.6 4.8 %all-to-all-start = ((bf16[4,1,2]{2,1,0:T(2,128)(2,1)}), bf16[4,1,2]{2,1,0:T(2,128)(2,1)S(1)}, u32[]{:S(2)}, u32[]{:S(2)}) async-start(bf16[4,1,2]{2,1,0:T(2,128)(2,1)} %and_convert_fusion), calls=%async_computation | async-start | bytes 4096 | tf_op jit(solution)/shard_map/all_to_all | solution.py:120
  258.4 75.9 %reduce-scatter.2.cloned.1.call-done = f32[128,4096]{1,0:T(8,128)} async-done(((f32[512,4096]{1,0:T(8,128)}), f32[128,4096]{1,0:T(8,128)}) %reduce-scatter.2.cloned.1.call-update) | async-done | bytes 2097168 | tf_op jit(solution)/shard_map/reduce_scatter | solution.py:94
  334.4 2.1 multiply_reduce_fusion
  336.5 85.2 %all-gather.8.cloned.1.call-done = bf16[4096,1024]{1,0:T(8,128)(2,1)} async-done(((bf16[64,1024]{1,0:T(8,128)(2,1)}), bf16[4096,1024]{1,0:T(8,128)(2,1)}) %all-gather.8.cloned.1.call-update) | async-done | bytes 8388624 | tf_op jit(solution)/shard_map/all_gather | solution.py:110
  421.6 4.7 %convolution_convert_fusion.1 = bf16[128,1024]{1,0:T(8,128)(2,1)S(1)} fusion(bf16[4096,1024]{1,0:T(8,128)(2,1)} %all-gather.8.cloned.1.call-done, f32[128,4096]{1,0:T(8,128)S(1)} %copy-done.2, bf16[128,4096]{1,0:T(8,128)(2,1)S(1)} %copy-done.3, f32[4096]{0:T(1024)S(1)} %copy-done.7, f32[128]{0:T(128)S(1)} %add_rsqrt_fusion), kind=kOutput, calls=%fused_computation.20 | convolution fusion | flops 1076494336 | bytes 11813376 | tf_op jit(solution)/shard_map/dot_general | solution.py:108
  426.3 0.0 copy-start.1
  426.3 1.1 broadcast_select_fusion
  427.5 0.0 all-to-all-done
  427.5 4.8 %all-to-all-start.1 = ((bf16[4,1,128,1024]{3,2,1,0:T(8,128)(2,1)}), bf16[4,1,128,1024]{3,2,1,0:T(8,128)(2,1)S(1)}, u32[]{:S(2)}, u32[]{:S(2)}) async-start(bf16[4,1,128,1024]{3,2,1,0:T(8,128)(2,1)} %broadcast_select_fusion), calls=%async_computation.2 | async-start | bytes 2097152 | tf_op jit(solution)/shard_map/all_to_all | solution.py:119
  432.2 0.1 copy.34
  432.4 13.3 %all-to-all-done.1 = bf16[4,1,128,1024]{3,2,1,0:T(8,128)(2,1)S(1)} async-done(((bf16[4,1,128,1024]{3,2,1,0:T(8,128)(2,1)}), bf16[4,1,128,1024]{3,2,1,0:T(8,128)(2,1)S(1)}, u32[]{:S(2)}, u32[]{:S(2)}) %all-to-all-start.1) | async-done | bytes 1048608 | tf_op jit(solution)/shard_map/all_to_all | solution.py:119
  445.7 0.9 fusion.9
  446.6 0.9 copy.42
  (23 shorter events, 0.1 us)
Async XLA Ops:
  6.5 150.9 %copy-start = (bf16[512,1024]{1,0:T(8,128)(2,1)S(1)}, bf16[512,1024]{1,0:T(8,128)(2,1)}, u32[]{:S(2)}) copy-start(bf16[512,1024]{1,0:T(8,128)(2,1)} %param.11) | copy-start | bytes 3145732
  6.5 4.4 copy-start.5
  6.5 150.9 %all-gather.10.cloned.1.call-start = ((), (), s32[]{:S(2)}) async-start(), calls=%async_computation.6 | async-start | bytes 34078720 | tf_op jit(solution)/shard_map/all_gather | solution.py:13
  11.0 141.2 %copy-start.6 = (bf16[512,1024]{0,1:T(8,128)(2,1)}, bf16[512,1024]{0,1:T(8,128)(2,1)S(1)}, u32[]{:S(2)}) copy-start(bf16[512,1024]{0,1:T(8,128)(2,1)S(1)} %copy.46) | copy-start | bytes 3145732
  11.0 2.1 copy-start.9
  12.3 227.8 %all-gather.6.cloned.1.call-start = ((), (), s32[]{:S(2)}) async-start(), calls=%async_computation.3 | async-start | bytes 8519680 | tf_op jit(solution)/shard_map/all_gather | solution.py:91
  13.1 321.3 %reduce-scatter.2.cloned.1.call-start = ((), (), s32[]{:S(2)}) async-start(), calls=%async_computation.4 | async-start | bytes 10485760 | tf_op jit(solution)/shard_map/reduce_scatter | solution.py:94
  159.9 7.5 %copy-start.4 = (f32[8,128,512]{2,1,0:T(8,128)S(1)}, f32[8,128,512]{2,1,0:T(8,128)}, u32[]{:S(2)}) copy-start(f32[8,128,512]{2,1,0:T(8,128)} %fusion.11) | copy-start | bytes 6291460
  250.4 0.7 copy-start.8
  250.4 84.0 %copy-start.3 = (bf16[128,4096]{1,0:T(8,128)(2,1)S(1)}, bf16[128,4096]{1,0:T(8,128)(2,1)}, u32[]{:S(2)}) copy-start(bf16[128,4096]{1,0:T(8,128)(2,1)} %param.15) | copy-start | bytes 3145732
  250.4 171.2 %copy-start.7 = (f32[4096]{0:T(1024)S(1)}, f32[4096]{0:T(1024)}, u32[]{:S(2)}) copy-start(f32[4096]{0:T(1024)} %param.17) | copy-start | bytes 49156
  250.4 171.2 %all-gather.8.cloned.1.call-start = ((), (), s32[]{:S(2)}) async-start(), calls=%async_computation.5 | async-start | bytes 8519680 | tf_op jit(solution)/shard_map/all_gather | solution.py:110
  253.6 173.8 %all-to-all-start = ((bf16[4,1,2]{2,1,0:T(2,128)(2,1)}), bf16[4,1,2]{2,1,0:T(2,128)(2,1)S(1)}, u32[]{:S(2)}, u32[]{:S(2)}) async-start(bf16[4,1,2]{2,1,0:T(2,128)(2,1)} %and_convert_fusion), calls=%async_computation | async-start | bytes 4096 | tf_op jit(solution)/shard_map/all_to_all | solution.py:120
  334.4 87.3 %copy-start.2 = (f32[128,4096]{1,0:T(8,128)S(1)}, f32[128,4096]{1,0:T(8,128)}, u32[]{:S(2)}) copy-start(f32[128,4096]{1,0:T(8,128)} %reduce-scatter.2.cloned.1.call-done) | copy-start | bytes 6291460
  426.3 21.2 %copy-start.1 = (bf16[512,1024]{1,0:T(8,128)(2,1)S(1)}, bf16[512,1024]{1,0:T(8,128)(2,1)}, u32[]{:S(2)}) copy-start(bf16[512,1024]{1,0:T(8,128)(2,1)} %param.11) | copy-start | bytes 3145732
  427.5 18.2 %all-to-all-start.1 = ((bf16[4,1,128,1024]{3,2,1,0:T(8,128)(2,1)}), bf16[4,1,128,1024]{3,2,1,0:T(8,128)(2,1)S(1)}, u32[]{:S(2)}, u32[]{:S(2)}) async-start(bf16[4,1,128,1024]{3,2,1,0:T(8,128)(2,1)} %broadcast_select_fusion), calls=%async_computation.2 | async-start | bytes 2097152 | tf_op jit(solution)/shard_map/all_to_all | solution.py:119
Sparse Core Ops, SparseCore 0:
  12.4 144.9 all-gather.9
  160.2 79.8 all-gather.5
  250.5 83.7 reduce-scatter.1
  337.0 84.6 all-gather.7
where the time goes:
time: 459 us; the launch traced here: 454 us
  waiting for transfers between devices  252 us (55%)
  blocking collectives  136 us (30%)
  matrix products  27 us (6%)
  between operations  13.9 us (3%)
  other arithmetic  10 us (2%)
  starting transfers between devices  9.71 us (2%)
  local copies, waits for them, and re-layouts  5.8 us (1%)
    unnamed x1, blocking collectives  136 us
    all_gather x1, waiting for transfers between devices, on_device(): lax.all_gather(kv_weight, 'seq', axis=0, tiled=True)  85.2 us
    reduce_scatter x1, waiting for transfers between devices, on_device(): lax.psum_scatter(partial_value, 'pool', scatter_dimension=0, tiled=True)  75.9 us
    all_gather x1, waiting for transfers between devices, on_device(): lax.all_gather(out_weight, 'seq', axis=1, tiled=True)  70.6 us
    all_to_all x1, waiting for transfers between devices, on_device(): lax.all_to_all(outgoing, 'pool', split_axis=0, concat_axis=0, tiled=True)  13.3 us
    dot_general x1, matrix products, on_device(): jnp.dot(mixed_list, lax.all_gather(out_weight, 'seq', axis=1, tiled=True)...  10.3 us
  transfers between devices with their start and end apart: 6, of which 5 were waited for; matrix products, arithmetic and copies ran while one was open for 5% of the time, Pallas kernels for 0%

commit v1 on v0

v1 whole, which is shorter than its diff:
```python
import jax
import jax.numpy as jnp
from jax import lax
from jax.experimental import pallas as pl
from jax.experimental.pallas import tpu as pltpu
from jax.sharding import PartitionSpec as P

NY, NZ, NX = 4, 8, 4
HEADS = 8
HD = 128
BLK = 512
PAGE = 128
D = 4096
KVW = 1024
CH = 8
CW = D // CH
DW = CW // 2
NT = 4
TW = KVW // NT
F32 = jnp.float32
BF16 = jnp.bfloat16
MESH = pl.DeviceIdType.MESH
NT_DIMS = (((1,), (1,)), ((), ()))
TN_DIMS = (((0,), (0,)), ((), ()))
HIGH = lax.Precision.HIGHEST


def kernel(
    wt, kw, q_hbm, k_hbm, v_hbm, ld, res_hbm, gain, tbl,
    pages, tables,
    gw, gk, q_s, k_s, v_s, res_s, crow, ccol, a_s, a_r, u_s, inner, mixed,
    ub_s, ub_r, st_s, st_r, sr_s, sr_r, se_s, se_r, sf_s, sf_r, state,
    part, rs_s, rs_r, hid, norm, pg, tb,
    ld_sem, w_zs, w_ys, w_fs, w_ps, w_r, w_p,
    k_zs, k_ys, k_fs, k_ps, k_r, k_h, k_p,
    s1_s, s1_r, s2_s, s2_r, s3_s, s3_r, s4_s, s4_r, s5_s, s5_r,
    rs_ss, rs_rs, g_s, g_f, g_r, t_s, t_r,
):
    me = lax.axis_index("seq")
    x = lax.axis_index("pool")
    y = lax.div(me, 16)
    z = lax.rem(lax.div(me, 2), 8)
    c = lax.rem(me, 2)

    def at(yy, zz, cc):
        return (yy * NZ + zz) * 2 + cc

    def mod(value, size):
        return lax.rem(value + size, size)

    up = (at(mod(y + 1, NY), z, c), x)
    down = (at(mod(y - 1, NY), z, c), x)
    ahead = (at(y, mod(z + 1, NZ), c), x)
    behind = (at(y, mod(z - 1, NZ), c), x)
    partner = (at(y, z, 1 - c), x)
    right = (me, mod(x + 1, NX))
    left = (me, mod(x - 1, NX))

    def send(src, dst, ssem, rsem, device):
        copy = pltpu.make_async_remote_copy(
            src_ref=src, dst_ref=dst, send_sem=ssem, recv_sem=rsem,
            device_id=device, device_id_type=MESH,
        )
        return copy

    def arrive(ref, rsem):
        send(ref, ref, rsem, rsem, partner).wait_recv()

    def sent(ref, ssem):
        send(ref, ref, ssem, ssem, partner).wait_send()

    peers = [partner]
    peers += [(at(y, mod(z + m, NZ), c), x) for m in range(1, NZ)]
    peers += [(at(mod(y + m, NY), z, c), x) for m in range(1, NY)]
    peers += [(me, mod(x + m, NX)) for m in range(1, NX)]
    barrier = pltpu.get_barrier_semaphore()
    for peer in peers:
        pl.semaphore_signal(barrier, inc=1, device_id=peer, device_id_type=MESH)
    loads = [
        pltpu.make_async_copy(k_hbm, k_s, ld_sem.at[0]),
        pltpu.make_async_copy(v_hbm, v_s, ld_sem.at[1]),
        pltpu.make_async_copy(q_hbm, q_s, ld_sem.at[2]),
        pltpu.make_async_copy(res_hbm, res_s, ld_sem.at[3]),
        pltpu.make_async_copy(wt, gw.at[me], ld_sem.at[4]),
        pltpu.make_async_copy(kw, gk.at[me], ld_sem.at[5]),
    ]
    for load in loads:
        load.start()
    pl.semaphore_wait(barrier, len(peers))

    def near(i):
        half = lax.div(i + 1, 2)
        return mod(z + half * (1 - 2 * lax.rem(i, 2)), NZ)

    row_step = (0, 3, 1, 2)

    def slot(r, i):
        return at(mod(y + row_step[r], NY), near(i), c)

    def w_rows(src, s, i):
        send(src, gw.at[s], w_ys.at[0, i], w_r.at[1, i], up).start()
        send(src, gw.at[s], w_ys.at[1, i], w_r.at[2, i], down).start()

    def w_pass(src, s, r, i):
        send(src, gw.at[s], w_ps.at[r, i], w_p.at[r, i], partner).start()

    def w_start():
        send(wt, gw.at[me], w_zs.at[0, 0], w_r.at[0, 1], ahead).start()
        send(wt, gw.at[me], w_zs.at[1, 0], w_r.at[0, 2], behind).start()
        w_rows(wt, me, 0)
        w_pass(wt, me, 0, 0)

    def w_along(i):
        s = slot(0, i)
        odd = lax.rem(i, 2)
        arrive(gw.at[s], w_r.at[0, i])

        @pl.when(i <= 5)
        def _():
            target = (at(y, mod(z + 2 * odd - 1, NZ), c), x)
            send(
                gw.at[s], gw.at[s], w_zs.at[1 - odd, lax.div(i + 1, 2)],
                w_r.at[0, i + 2], target,
            ).start()

        w_rows(gw.at[s], s, i)
        w_pass(gw.at[s], s, 0, i)

    def w_across(i):
        below, above = slot(1, i), slot(2, i)
        even = lax.rem(i, 2) == 0
        arrive(gw.at[below], w_r.at[1, i])
        arrive(gw.at[above], w_r.at[2, i])
        s = jnp.where(even, below, above)
        target = (jnp.where(even, up[0], down[0]), x)
        send(gw.at[s], gw.at[s], w_fs.at[i], w_r.at[3, i], target).start()
        w_pass(gw.at[below], below, 1, i)
        w_pass(gw.at[above], above, 2, i)

    def w_last(i):
        s = slot(3, i)
        arrive(gw.at[s], w_r.at[3, i])
        w_pass(gw.at[s], s, 3, i)

    def k_along(src, s, r):
        send(src, gk.at[s], k_zs.at[0, r, 0], k_r.at[r, 1], ahead).start()
        send(src, gk.at[s], k_zs.at[1, r, 0], k_r.at[r, 2], behind).start()
        send(src, gk.at[s], k_ps.at[r, 0], k_p.at[r, 0], partner).start()

    def k_start():
        send(kw, gk.at[me], k_ys.at[0], k_r.at[1, 0], up).start()
        send(kw, gk.at[me], k_ys.at[1], k_r.at[2, 0], down).start()
        k_along(kw, me, 0)

    def k_across():
        below, above = slot(1, 0), slot(2, 0)
        arrive(gk.at[below], k_r.at[1, 0])
        arrive(gk.at[above], k_r.at[2, 0])
        low = gk.at[below, pl.ds(0, 32)]
        top = gk.at[above, pl.ds(32, 32)]
        send(low, low, k_fs.at[0], k_h.at[0], up).start()
        send(top, top, k_fs.at[1], k_h.at[1], down).start()
        k_along(gk.at[below], below, 1)
        k_along(gk.at[above], above, 2)

    def k_last():
        s = slot(3, 0)
        arrive(gk.at[s, pl.ds(0, 32)], k_h.at[0])
        arrive(gk.at[s, pl.ds(32, 32)], k_h.at[1])
        k_along(gk.at[s], s, 3)

    def k_ring(i):
        odd = lax.rem(i, 2)
        for r in range(NY):
            s = slot(r, i)
            arrive(gk.at[s], k_r.at[r, i])

            @pl.when(i <= 5)
            def _():
                target = (at(y, mod(z + 2 * odd - 1, NZ), c), x)
                send(
                    gk.at[s], gk.at[s], k_zs.at[1 - odd, r, lax.div(i + 1, 2)],
                    k_r.at[r, i + 2], target,
                ).start()

            send(gk.at[s], gk.at[s], k_ps.at[r, i], k_p.at[r, i], partner).start()

    w_start()
    for m in range(1, NX):
        target = (me, mod(x + m, NX))
        send(tbl, tb.at[x], t_s.at[m - 1], t_r.at[m - 1], target).start()

    steps_a = lax.broadcasted_iota(jnp.int32, (BLK, BLK), 0)
    steps_b = lax.broadcasted_iota(jnp.int32, (BLK, BLK), 1)
    lower = jnp.where(steps_b <= steps_a, 1.0, 0.0).astype(F32)
    decay = ld[...]
    sums_row = lax.dot_general(decay, lower, NT_DIMS, precision=HIGH, preferred_element_type=F32)
    sums_col = lax.dot_general(lower, decay, NT_DIMS, precision=HIGH, preferred_element_type=F32)
    for h in range(HEADS):
        crow[h] = sums_row[h : h + 1, :]
        wide = jnp.broadcast_to(sums_col[:, h : h + 1], (BLK, HD))
        ccol[h] = wide
        a_s[h] = jnp.broadcast_to(wide[BLK - 1 : BLK, :], (8, HD))

    def head_cols(h):
        return pl.ds(pl.multiple_of(h * HD, HD), HD)

    loads[0].wait()
    loads[1].wait()

    def update(h, carry):
        cb = ccol[h]
        gap = jnp.exp(cb[BLK - 1 : BLK, :] - cb)
        weighted = (k_s[:, head_cols(h)].astype(F32) * gap).astype(BF16)
        u_s[h] = lax.dot_general(
            weighted, v_s[:, head_cols(h)], TN_DIMS, preferred_element_type=F32
        )
        return carry

    lax.fori_loop(0, HEADS, update, 0)
    ub_s[...] = u_s[pl.ds(4 * (1 - c), 4)].astype(BF16)
    send(ub_s, ub_r, s1_s.at[0], s1_r.at[0], partner).start()
    send(a_s, a_r, s1_s.at[1], s1_r.at[1], partner).start()

    def chip_parts():
        own = u_s[pl.ds(4 * c, 4)]
        other = ub_r[...].astype(F32)
        a_own = a_s[pl.ds(4 * c, 4)]
        a_other = a_r[pl.ds(4 * c, 4)]
        first = c == 0
        return (
            jnp.where(first, own, other),
            jnp.where(first, other, own),
            jnp.where(first, a_own, a_other),
            jnp.where(first, a_other, a_own),
        )

    def scan_chip():
        arrive(ub_r, s1_r.at[0])
        arrive(a_r, s1_r.at[1])
        u0, u1, a0, a1 = chip_parts()
        total = jnp.exp(a1)[:, 0:1, :] * u0 + u1
        a_chip = a0 + a1
        rows = lax.broadcasted_iota(jnp.int32, (16, HD), 0)
        for hl in range(4):
            a = jnp.broadcast_to(a_chip[hl, 0:1, :], (16, HD))
            hi = a.astype(BF16).astype(F32)
            mid = (a - hi).astype(BF16).astype(F32)
            low = a - hi - mid
            tile = jnp.where(rows == 0, hi, jnp.where(rows == 1, mid, jnp.where(rows == 2, low, 0.0)))
            for half in range(2):
                st_s[2 * hl + half, 0:64, :] = total[hl, 64 * half : 64 * half + 64, :].astype(BF16)
                st_s[2 * hl + half, 64:80, :] = tile.astype(BF16)
        st_r[z] = st_s[z]
        for m in range(1, NZ):
            zz = mod(z + m, NZ)
            send(st_s.at[zz], st_r.at[z], s2_s.at[m], s2_r.at[m], (at(y, zz, c), x)).start()

    def chip_total(zz):
        message = st_r[zz].astype(F32)
        return message[0:64, :], jnp.sum(message[64:80, :], axis=0, keepdims=True)

    def scan_row():
        for m in range(1, NZ):
            arrive(st_r.at[mod(z - m, NZ)], s2_r.at[m])
        total = jnp.zeros((64, HD), F32)
        a_row = jnp.zeros((1, HD), F32)
        for zz in range(NZ):
            t, a = chip_total(zz)
            total = jnp.exp(a) * total + t
            a_row = a_row + a
        sr_s[0:64, :] = total
        sr_s[64:72, :] = jnp.broadcast_to(a_row, (8, HD))
        sr_r[y] = sr_s[...]
        for m in range(1, NY):
            target = (at(mod(y + m, NY), z, c), x)
            send(sr_s, sr_r.at[y], s3_s.at[m], s3_r.at[m], target).start()

    def scan_back():
        for m in range(1, NY):
            arrive(sr_r.at[mod(y - m, NY)], s3_r.at[m])
        enter = jnp.zeros((64, HD), F32)
        for yy in range(NY):
            moved = jnp.exp(sr_r[yy, 64:65, :]) * enter + sr_r[yy, 0:64, :]
            enter = jnp.where(yy < y, moved, enter)
        for zz in range(NZ):
            se_s[zz] = enter.astype(BF16)
            t, a = chip_total(zz)
            enter = jnp.exp(a) * enter + t
        se_r[z] = se_s[z]
        for m in range(1, NZ):
            zz = mod(z + m, NZ)
            send(se_s.at[zz], se_r.at[z], s4_s.at[m], s4_r.at[m], (at(y, zz, c), x)).start()

    def scan_cores():
        for m in range(1, NZ):
            arrive(se_r.at[mod(z - m, NZ)], s4_r.at[m])
        enter = se_r[...].reshape(4, HD, HD).astype(F32)
        u0, _, a0, _ = chip_parts()
        after = jnp.exp(a0)[:, 0:1, :] * enter + u0
        first = c == 0
        sf_s[...] = jnp.where(first, after, enter).astype(BF16)
        send(sf_s, sf_r, s5_s.at[0], s5_r.at[0], partner).start()
        state[pl.ds(4 * c, 4)] = jnp.where(first, enter, after).astype(BF16)

    loads[2].wait()
    loads[4].wait()
    loads[5].wait()

    tri_a = lax.broadcasted_iota(jnp.int32, (HD, HD), 0)
    tri_b = lax.broadcasted_iota(jnp.int32, (HD, HD), 1)
    seen = tri_b <= tri_a

    def within(h, carry):
        @pl.when(h == 1)
        def _():
            scan_chip()

        @pl.when(h == 4)
        def _():
            scan_row()

        @pl.when(h == 5)
        def _():
            k_start()

        @pl.when(h == 6)
        def _():
            scan_back()

        for tq in range(4):
            rows = pl.ds(tq * HD, HD)
            width = HD * (tq + 1)
            products = lax.dot_general(
                q_s[rows, head_cols(h)], k_s[0:width, head_cols(h)], NT_DIMS,
                preferred_element_type=F32,
            )
            c_here = ccol[h, rows, :]
            blocks = []
            for ts in range(tq + 1):
                gap = c_here - crow[h, :, ts * HD : ts * HD + HD]
                piece = products[:, ts * HD : ts * HD + HD]
                if ts == tq:
                    gap = jnp.where(seen, gap, 0.0)
                    piece = jnp.where(seen, piece, 0.0)
                blocks.append((piece * jnp.exp(gap)).astype(BF16))
            scores = jnp.concatenate(blocks, axis=1) if tq else blocks[0]
            inner[rows, head_cols(h)] = jnp.dot(
                scores, v_s[0:width, head_cols(h)], preferred_element_type=F32
            )

        @pl.when(h >= 1)
        def _():
            w_along(h)

        return carry

    lax.fori_loop(0, HEADS, within, 0)
    scan_cores()
    w_across(0)
    w_across(1)
    arrive(sf_r, s5_r.at[0])
    state[pl.ds(4 * (1 - c), 4)] = sf_r[...]

    def finish(h, carry):
        outer = jnp.dot(q_s[:, head_cols(h)], state[h], preferred_element_type=F32)
        kept = inner[:, head_cols(h)] + outer * jnp.exp(ccol[h])
        scale = lax.rsqrt(jnp.mean(kept * kept, axis=-1, keepdims=True) + 1e-05)
        mixed[:, head_cols(h)] = (kept * scale).astype(BF16)
        return carry

    lax.fori_loop(0, HEADS, finish, 0)
    loads[3].wait()

    def row_of(r):
        step = jnp.where(r == 1, 3, jnp.where(r == 2, 1, jnp.where(r == 3, 2, 0)))
        return mod(y + step, NY)

    def chunk_rows(j):
        return row_of(lax.div(j, 2)) * 16 + lax.rem(j, 2) * 8

    def direction(d):
        return (right, -1) if d == 0 else (left, 1)

    def forward(j, step, d, value):
        rs_s[d, j, step] = value.astype(BF16)
        send(
            rs_s.at[d, j, step], rs_r.at[d, j, step],
            rs_ss.at[d, j, step], rs_rs.at[d, j, step], direction(d)[0],
        ).start()

    def w_ready(r):
        for i in range(NZ):
            s = at(row_of(r), near(i), 1 - c)
            arrive(gw.at[s], w_p.at[r, i])

    def reduce(t, carry):
        @pl.when(t == 0)
        def _():
            w_ready(0)

        @pl.when(t < CH)
        def _():
            weight = gw[pl.ds(chunk_rows(t), 8)].reshape(CW, HEADS * HD)
            product = lax.dot_general(mixed[...], weight, NT_DIMS, preferred_element_type=F32)
            part[t] = product.reshape(NX, PAGE, CW)
            for d in range(2):
                block = mod(x + direction(d)[1], NX)
                forward(t, 0, d, part[t, block, :, d * DW : d * DW + DW])

        for step in (1, 2):

            @pl.when(jnp.logical_and(t >= step, t < CH + step))
            def _():
                j = t - step
                for d in range(2):
                    arrive(rs_r.at[d, j, step - 1], rs_rs.at[d, j, step - 1])
                    block = lax.rem(x + direction(d)[1] * (1 + step) + 2 * NX, NX)
                    own = part[j, block, :, d * DW : d * DW + DW]
                    forward(j, step, d, rs_r[d, j, step - 1].astype(F32) + own)

        @pl.when(t >= 3)
        def _():
            j = t - 3
            for d in range(2):
                arrive(rs_r.at[d, j, 2], rs_rs.at[d, j, 2])
                own = part[j, x, :, d * DW : d * DW + DW]
                cols = pl.ds(pl.multiple_of(chunk_rows(j) * 64 + d * DW, DW), DW)
                hid[:, cols] = rs_r[d, j, 2].astype(F32) + own + res_s[:, cols].astype(F32)

        @pl.when(t == 0)
        def _():
            k_across()
            for i in (2, 3, 4):
                w_across(i)

        @pl.when(t == 1)
        def _():
            k_last()
            for i in (5, 6, 7):
                w_across(i)
            w_ready(1)

        @pl.when(jnp.logical_and(t >= 2, t < 4))
        def _():
            for i in range(4):
                w_last(4 * (t - 2) + i)

        @pl.when(t == 3)
        def _():
            w_ready(2)

        @pl.when(t == 5)
        def _():
            w_ready(3)

        @pl.when(jnp.logical_and(t >= 2, t < 9))
        def _():
            k_ring(t - 1)

        return carry

    lax.fori_loop(0, CH + 3, reduce, 0)

    def square(j, total):
        cols = pl.ds(pl.multiple_of(j * CW, CW), CW)
        value = hid[:, cols]
        return total + jnp.sum(value * value, axis=-1, keepdims=True)

    squares = lax.fori_loop(0, CH, square, jnp.zeros((PAGE, 1), F32))
    scale = lax.rsqrt(squares * (1.0 / D) + 1e-05)

    def normalize(j, carry):
        cols = pl.ds(pl.multiple_of(j * CW, CW), CW)
        norm[:, cols] = (hid[:, cols] * scale * gain[:, cols]).astype(BF16)
        return carry

    lax.fori_loop(0, CH, normalize, 0)

    def k_ready(i, carry):
        for r in range(NY):
            s = at(row_of(r), near(i), 1 - c)
            arrive(gk.at[s], k_p.at[r, i])
        return carry

    lax.fori_loop(0, NZ, k_ready, 0)
    x_left = mod(x - 1, NX)
    x_right = mod(x + 1, NX)
    x_far = mod(x + 2, NX)

    def tile(n):
        return pl.ds(pl.multiple_of(n * TW, TW), TW)

    def project(n, carry):
        @pl.when(n < NT)
        def _():
            weight = gk[:, :, tile(n)].reshape(D, TW)
            value = jnp.dot(norm[...], weight, preferred_element_type=F32)
            pg[x, :, tile(n)] = value.astype(BF16)
            own = pg.at[x, :, tile(n)]
            send(own, own, g_s.at[0, n], g_r.at[0, n], right).start()
            send(own, own, g_s.at[1, n], g_r.at[1, n], left).start()

        @pl.when(n >= 2)
        def _():
            j = n - 2
            arrive(pg.at[x_left, :, tile(j)], g_r.at[0, j])
            arrive(pg.at[x_right, :, tile(j)], g_r.at[1, j])
            early = j < 2
            source = jnp.where(early, x_left, x_right)
            target = (me, jnp.where(early, right[1], left[1]))
            page = pg.at[source, :, tile(j)]
            send(page, page, g_f.at[j], g_r.at[2, j], target).start()

        return carry

    lax.fori_loop(0, NT + 2, project, 0)

    def drain_w(i, carry):
        for d in range(2):
            sent(gw.at[0], w_ys.at[d, i])
        sent(gw.at[0], w_fs.at[i])
        for r in range(NY):
            sent(gw.at[0], w_ps.at[r, i])
            sent(gk.at[0], k_ps.at[r, i])
        return carry

    lax.fori_loop(0, NZ, drain_w, 0)
    for d, count in ((0, 4), (1, 3)):
        for n in range(count):
            sent(gw.at[0], w_zs.at[d, n])
            for r in range(NY):
                sent(gk.at[0], k_zs.at[d, r, n])
    for d in range(2):
        sent(gk.at[0], k_ys.at[d])
        sent(gk.at[0, pl.ds(0, 32)], k_fs.at[d])
    sent(ub_s, s1_s.at[0])
    sent(a_s, s1_s.at[1])
    sent(sf_s, s5_s.at[0])
    for m in range(1, NZ):
        sent(st_s.at[0], s2_s.at[m])
        sent(se_s.at[0], s4_s.at[m])
    for m in range(1, NY):
        sent(sr_s, s3_s.at[m])

    def drain_rs(j, carry):
        for d in range(2):
            for step in range(3):
                sent(rs_s.at[0, 0, 0], rs_ss.at[d, j, step])
        return carry

    lax.fori_loop(0, CH, drain_rs, 0)
    tb[x] = tbl[...]
    for m in range(1, NX):
        arrive(tb.at[mod(x - m, NX)], t_r.at[m - 1])
        sent(tbl, t_s.at[m - 1])
    tables[...] = tb[...]
    for n in range(NT):
        sent(pg.at[0, :, pl.ds(0, TW)], g_s.at[0, n])
        sent(pg.at[0, :, pl.ds(0, TW)], g_s.at[1, n])
        sent(pg.at[0, :, pl.ds(0, TW)], g_f.at[n])
    for n in range(NT):
        arrive(pg.at[x_far, :, tile(n)], g_r.at[2, n])
    pages[...] = pg[...]


def on_device(query_rows, key_rows, value_rows, log_decay, residual, out_weight, norm_gain, kv_weight, block_table):
    vm, dma = pltpu.VMEM, pltpu.SemaphoreType.DMA
    table = jnp.broadcast_to(block_table.reshape(2, 1, 1), (2, 8, HD))
    hbm = pl.BlockSpec(memory_space=pl.ANY)
    vmem = pl.BlockSpec(memory_space=pltpu.VMEM)
    pages, tables = pl.pallas_call(
        kernel,
        out_shape=(
            jax.ShapeDtypeStruct((NX, PAGE, KVW), BF16),
            jax.ShapeDtypeStruct((NX, 2, 8, HD), jnp.int32),
        ),
        in_specs=[hbm, hbm, hbm, hbm, hbm, vmem, hbm, vmem, vmem],
        out_specs=(vmem, vmem),
        scratch_shapes=[
            vm((64, 64, HEADS * HD), BF16),
            vm((64, 64, KVW), BF16),
            vm((BLK, HEADS * HD), BF16),
            vm((BLK, HEADS * HD), BF16),
            vm((BLK, HEADS * HD), BF16),
            vm((PAGE, D), BF16),
            vm((HEADS, 1, BLK), F32),
            vm((HEADS, BLK, HD), F32),
            vm((HEADS, 8, HD), F32),
            vm((HEADS, 8, HD), F32),
            vm((HEADS, HD, HD), F32),
            vm((BLK, HEADS * HD), F32),
            vm((BLK, HEADS * HD), BF16),
            vm((4, HD, HD), BF16),
            vm((4, HD, HD), BF16),
            vm((NZ, 80, HD), BF16),
            vm((NZ, 80, HD), BF16),
            vm((72, HD), F32),
            vm((NY, 72, HD), F32),
            vm((NZ, 64, HD), BF16),
            vm((NZ, 64, HD), BF16),
            vm((4, HD, HD), BF16),
            vm((4, HD, HD), BF16),
            vm((HEADS, HD, HD), BF16),
            vm((CH, NX, PAGE, CW), F32),
            vm((2, CH, 3, PAGE, DW), BF16),
            vm((2, CH, 3, PAGE, DW), BF16),
            vm((PAGE, D), F32),
            vm((PAGE, D), BF16),
            vm((NX, PAGE, KVW), BF16),
            vm((NX, 2, 8, HD), jnp.int32),
            dma((6,)),
            dma((2, 4)), dma((2, NZ)), dma((NZ,)), dma((NY, NZ)), dma((NY, NZ)), dma((NY, NZ)),
            dma((2, NY, 4)), dma((2,)), dma((2,)), dma((NY, NZ)), dma((NY, NZ)), dma((2,)), dma((NY, NZ)),
            dma((2,)), dma((2,)), dma((NZ,)), dma((NZ,)), dma((NY,)), dma((NY,)),
            dma((NZ,)), dma((NZ,)), dma((1,)), dma((1,)),
            dma((2, CH, 3)), dma((2, CH, 3)), dma((2, NT)), dma((NT,)), dma((3, NT)), dma((3,)), dma((3,)),
        ],
        compiler_params=pltpu.CompilerParams(
            collective_id=0, has_side_effects=True, vmem_limit_bytes=63 * 1024 * 1024
        ),
        name="layer",
    )(
        out_weight.T, kv_weight, query_rows, key_rows, value_rows, log_decay,
        residual, norm_gain.reshape(1, D), table,
    )
    mine = tables[:, 0, 0, 0] == lax.axis_index("pool")
    slot = tables[:, 1, 0, 0]
    slots = []
    for s in range(2):
        total = jnp.zeros((PAGE, KVW), BF16)
        for p in range(NX):
            total = jnp.where(jnp.logical_and(mine[p], slot[p] == s), pages[p], total)
        slots.append(total)
    return jnp.stack(slots).reshape(1, 1, 2, PAGE, KVW)


def solution(mesh):
    placed = (
        P("seq", "pool"),
        P("seq", "pool"),
        P("seq", "pool"),
        P("pool", "seq"),
        P(("seq", "pool"), None),
        P("pool", "seq"),
        P(),
        P("seq", None),
        P(("seq", "pool"), None),
    )
    return jax.shard_map(
        on_device,
        mesh=mesh,
        in_specs=placed,
        out_specs=P("seq", "pool", None, None, None),
        check_vma=False,
    )
```

time: 459 us -> 127 us (0.28); the launches traced: 454 us -> 127 us
  waiting for transfers between devices: 252 us -> 0 us
  blocking collectives: 136 us -> 0 us
  Pallas kernels: 0 us -> 111 us
  matrix products: 27 us -> 0 us
  starting transfers between devices: 9.71 us -> 0 us
  other arithmetic: 10 us -> 2.83 us
    all_gather x3 -> x0, waiting for transfers between devices: 161 us -> none  [the longest x1 85.2 us: on_device(): lax.all_gather(kv_weight, 'seq', axis=0, tiled=True)]
    unnamed x1 -> x0, blocking collectives: 136 us -> none
    pallas_call x0 -> x1, Pallas kernels: none -> 111 us  [on_device(): pl.pallas_call(kernel, out_shape=(jax.ShapeDtypeStruct((NX, PAGE, KVW), B...]
    reduce_scatter x1 -> x0, waiting for transfers between devices: 75.9 us -> none  [on_device(): lax.psum_scatter(partial_value, 'pool', scatter_dimension=0, tiled=True)]
    dot_general x6 -> x0, matrix products: 27 us -> none  [the longest x1 10.3 us: on_device(): jnp.dot(mixed_list, lax.all_gather(out_weight, 'seq', axis=1, tiled=True)...]
    all_to_all x2 -> x0, waiting for transfers between devices: 13.3 us -> none  [the longest x1 13.3 us: on_device(): lax.all_to_all(outgoing, 'pool', split_axis=0, concat_axis=0, tiled=True)]
    all_to_all x2 -> x0, starting transfers between devices: 9.59 us -> none  [the longest x1 4.79 us: on_device(): lax.all_to_all(slot_tags, 'pool', split_axis=0, concat_axis=0, tiled=True)]
  transfers between devices with their start and end apart: 6 -> 0, of which waited for: 5 -> 0; matrix products, arithmetic and copies ran while one was open for 5% -> 0% of each run, Pallas kernels for 0% -> 0%
where the time goes in v1:
time: 127 us
  Pallas kernels  111 us (87%)
  between operations  10.1 us (8%)
  local copies, waits for them, and re-layouts  3.15 us (2%)
  other arithmetic  2.83 us (2%)
    pallas_call x1, Pallas kernels, on_device(): pl.pallas_call(kernel, out_shape=(jax.ShapeDtypeStruct((NX, PAGE, KVW), B...  111 us

profile of v1, /device:TPU:6, one launch (start us, length us, event | category | flops | bytes accessed | tf_op | source)
XLA Modules:
  0.0 127.0 jit_solution(8306877370685843894)
XLA Ops:
  0.0 0.0 copy-start
  0.0 0.7 copy-done
  0.7 0.7 broadcast_in_dim.8.tbl
  1.3 110.9 %layer.1 = (bf16[4,128,1024]{2,1,0:T(8,128)(2,1)}, s32[4,2,8,128]{3,2,1,0:T(8,128)}) custom-call(bf16[64,1024]{1,0:T(8,128)(2,1)} %bitcast.13, bf16[64,1024]{1,0:T(8,128)(2,1)} %kw.1, bf16[512,1024]{1,0:T(8,128)(2,1)} %q_hbm.1, bf16[512,1024]{1,0:T(8,128)(2,1)} %k_hbm.1, bf16[512,1024]{1,0:T(8,128)(2,1)} %v_hbm.1, f32[8,512]{1,0:T(8,128)} %ld.1, ...), custom_call_target="tpu_custom_call" | custom-call | tf_op jit(solution)/shard_map/layer/pallas_call | solution.py:572
  112.2 0.7 slice_compare_fusion
  113.0 1.3 %fusion = (s32[1,1,1,1]{3,2,1,0:T(1,128)}, s32[1,1,1,1]{3,2,1,0:T(1,128)}, s32[1,1,1,1]{3,2,1,0:T(1,128)}, s32[1,1,1,1]{3,2,1,0:T(1,128)}) fusion(s32[4,2,8,128]{3,2,1,0:T(8,128)} %get-tuple-element.7), kind=kLoop, calls=%fused_computation.4 | loop fusion | bytes 32 | tf_op jit(solution)/shard_map/slice | solution.py:633
  119.3 0.6 fusion.1
  124.9 1.3 select_select_fusion.1
  126.1 0.8 maximum_bitcast_fusion
Async XLA Ops:
  0.0 0.7 copy-start

commit v2 on v1

--- a/solution.py
+++ b/solution.py
@@ -27,10 +27,10 @@
 
 def kernel(
     wt, kw, q_hbm, k_hbm, v_hbm, ld, res_hbm, gain, tbl,
-    pages, tables,
+    cache,
     gw, gk, q_s, k_s, v_s, res_s, crow, ccol, a_s, a_r, u_s, inner, mixed,
     ub_s, ub_r, st_s, st_r, sr_s, sr_r, se_s, se_r, sf_s, sf_r, state,
-    part, rs_s, rs_r, hid, norm, pg, tb,
+    part, rs_s, rs_r, hid, norm, pg, tb, tb_s,
     ld_sem, w_zs, w_ys, w_fs, w_ps, w_r, w_p,
     k_zs, k_ys, k_fs, k_ps, k_r, k_h, k_p,
     s1_s, s1_r, s2_s, s2_r, s3_s, s3_r, s4_s, s4_r, s5_s, s5_r,
@@ -186,9 +186,11 @@
             send(gk.at[s], gk.at[s], k_ps.at[r, i], k_p.at[r, i], partner).start()
 
     w_start()
+    for n in range(2):
+        tb_s[n] = jnp.broadcast_to(tbl[0:1, n : n + 1], (8, HD))
     for m in range(1, NX):
         target = (me, mod(x + m, NX))
-        send(tbl, tb.at[x], t_s.at[m - 1], t_r.at[m - 1], target).start()
+        send(tb_s, tb.at[x], t_s.at[m - 1], t_r.at[m - 1], target).start()
 
     steps_a = lax.broadcasted_iota(jnp.int32, (BLK, BLK), 0)
     steps_b = lax.broadcasted_iota(jnp.int32, (BLK, BLK), 1)
@@ -550,33 +552,35 @@
         return carry
 
     lax.fori_loop(0, CH, drain_rs, 0)
-    tb[x] = tbl[...]
+    tb[x] = tb_s[...]
     for m in range(1, NX):
         arrive(tb.at[mod(x - m, NX)], t_r.at[m - 1])
-        sent(tbl, t_s.at[m - 1])
-    tables[...] = tb[...]
+        sent(tb_s, t_s.at[m - 1])
     for n in range(NT):
         sent(pg.at[0, :, pl.ds(0, TW)], g_s.at[0, n])
         sent(pg.at[0, :, pl.ds(0, TW)], g_s.at[1, n])
         sent(pg.at[0, :, pl.ds(0, TW)], g_f.at[n])
     for n in range(NT):
         arrive(pg.at[x_far, :, tile(n)], g_r.at[2, n])
-    pages[...] = pg[...]
+    here = [tb[p, 0] == x for p in range(NX)]
+    for s in range(2):
+        total = jnp.zeros((PAGE, KVW), BF16)
+        for p in range(NX):
+            hit = jnp.logical_and(here[p], tb[p, 1] == s).astype(F32)
+            hit = jnp.broadcast_to(hit[0:1, 0:1], (PAGE, KVW))
+            total = jnp.where(hit > 0.5, pg[p], total)
+        cache[s] = total
 
 
 def on_device(query_rows, key_rows, value_rows, log_decay, residual, out_weight, norm_gain, kv_weight, block_table):
     vm, dma = pltpu.VMEM, pltpu.SemaphoreType.DMA
-    table = jnp.broadcast_to(block_table.reshape(2, 1, 1), (2, 8, HD))
     hbm = pl.BlockSpec(memory_space=pl.ANY)
     vmem = pl.BlockSpec(memory_space=pltpu.VMEM)
-    pages, tables = pl.pallas_call(
+    cache = pl.pallas_call(
         kernel,
-        out_shape=(
-            jax.ShapeDtypeStruct((NX, PAGE, KVW), BF16),
-            jax.ShapeDtypeStruct((NX, 2, 8, HD), jnp.int32),
-        ),
+        out_shape=jax.ShapeDtypeStruct((2, PAGE, KVW), BF16),
         in_specs=[hbm, hbm, hbm, hbm, hbm, vmem, hbm, vmem, vmem],
-        out_specs=(vmem, vmem),
+        out_specs=vmem,
         scratch_shapes=[
             vm((64, 64, HEADS * HD), BF16),
             vm((64, 64, KVW), BF16),
@@ -609,6 +613,7 @@
             vm((PAGE, D), BF16),
             vm((NX, PAGE, KVW), BF16),
             vm((NX, 2, 8, HD), jnp.int32),
+            vm((2, 8, HD), jnp.int32),
             dma((6,)),
             dma((2, 4)), dma((2, NZ)), dma((NZ,)), dma((NY, NZ)), dma((NY, NZ)), dma((NY, NZ)),
             dma((2, NY, 4)), dma((2,)), dma((2,)), dma((NY, NZ)), dma((NY, NZ)), dma((2,)), dma((NY, NZ)),
@@ -622,17 +627,9 @@
         name="layer",
     )(
         out_weight.T, kv_weight, query_rows, key_rows, value_rows, log_decay,
-        residual, norm_gain.reshape(1, D), table,
+        residual, norm_gain.reshape(1, D), block_table,
     )
-    mine = tables[:, 0, 0, 0] == lax.axis_index("pool")
-    slot = tables[:, 1, 0, 0]
-    slots = []
-    for s in range(2):
-        total = jnp.zeros((PAGE, KVW), BF16)
-        for p in range(NX):
-            total = jnp.where(jnp.logical_and(mine[p], slot[p] == s), pages[p], total)
-        slots.append(total)
-    return jnp.stack(slots).reshape(1, 1, 2, PAGE, KVW)
+    return cache.reshape(1, 1, 2, PAGE, KVW)
 
 
 def solution(mesh):

time: 127 us -> 113 us (0.89)
  between operations: 10.1 us -> 0.01 us
  other arithmetic: 2.83 us -> 0 us
  local copies, waits for them, and re-layouts: 3.15 us -> 1.87 us
    slice x2 -> x0, local copies, waits for them, and re-layouts: 1.82 us -> none  [on_device(): total = jnp.where(jnp.logical_and(mine[p], slot[p] == s), pages[p], total)]
where the time goes in v2:
time: 113 us
  Pallas kernels  111 us (98%)
  local copies, waits for them, and re-layouts  1.87 us (2%)
    pallas_call x1, Pallas kernels, on_device(): pl.pallas_call(kernel, out_shape=jax.ShapeDtypeStruct((2, PAGE, KVW), BF1...  111 us

profile of v2, /device:TPU:6, one launch (start us, length us, event | category | flops | bytes accessed | tf_op | source)
XLA Modules:
  0.0 112.8 jit_solution(320809888262158759)
XLA Ops:
  0.0 110.9 %layer.1 = bf16[2,128,1024]{2,1,0:T(8,128)(2,1)} custom-call(bf16[64,1024]{1,0:T(8,128)(2,1)} %bitcast.4, bf16[64,1024]{1,0:T(8,128)(2,1)} %kw.1, bf16[512,1024]{1,0:T(8,128)(2,1)} %q_hbm.1, bf16[512,1024]{1,0:T(8,128)(2,1)} %k_hbm.1, bf16[512,1024]{1,0:T(8,128)(2,1)} %v_hbm.1, f32[8,512]{1,0:T(8,128)} %ld.1, bf16[128,4096]{1,0:T(8,128)(2,1)} %res_hbm.1, ...), custom_call_target="tpu_custom_call" | custom-call | tf_op jit(solution)/shard_map/layer/pallas_call | solution.py:579
  110.9 1.9 %copy.11 = bf16[1,1,2,128,1024]{4,3,2,1,0:T(8,128)(2,1)} copy(bf16[1,1,2,128,1024]{4,3,2,1,0:T(8,128)(2,1)} %bitcast.3) | data formatting | bytes 1048576

commit v3 on v2

--- a/solution.py
+++ b/solution.py
@@ -24,6 +24,39 @@
 TN_DIMS = (((0,), (0,)), ((), ()))
 HIGH = lax.Precision.HIGHEST
 
+PLAN = {
+    (0, 0): ((1, 0, 0, 1), (2, 0, 0, 2), (3, 0, 1, 0), (4, 0, 2, 0),),
+    (1, 0): ((3, 1, 1, 0), (4, 1, 2, 0),),
+    (2, 1, 1): ((0, 0, 0, 1), (0, 0, 0, 2), (0, 0, 1, 0), (0, 0, 2, 0), (3, 0, 1, 1), (4, 0, 2, 1),),
+    (2, 2, 2): ((2, 0, 0, 4),),
+    (2, 4, 2): ((0, 1, 1, 0), (0, 1, 2, 0), (3, 0, 1, 2), (4, 0, 2, 2), (1, 0, 0, 3),),
+    (2, 5, 0): ((0, 0, 1, 1), (0, 0, 2, 1), (3, 0, 3, 0), (4, 0, 3, 1), (0, 0, 0, 4), (2, 0, 0, 6),),
+    (2, 5, 1): ((0, 0, 1, 2), (0, 0, 2, 2),),
+    (2, 5, 2): ((0, 0, 0, 3), (1, 0, 0, 5), (4, 0, 2, 3),),
+    (2, 6, 2): ((3, 0, 1, 3),),
+    (2, 7, 2): ((0, 0, 3, 0), (0, 0, 3, 1),),
+    (3, 0): ((0, 0, 0, 6), (2, 0, 0, 7), (4, 0, 2, 4), (3, 0, 1, 4),),
+    (4, 0): ((0, 0, 0, 5), (0, 0, 2, 3), (4, 0, 2, 5), (0, 0, 1, 3), (3, 0, 1, 5), (2, 1, 0, 2), (0, 0, 0, 7), (1, 1, 0, 1), (0, 0, 2, 4), (4, 0, 2, 6), (0, 0, 1, 4), (3, 0, 1, 6), (2, 1, 1, 2), (1, 1, 1, 1), (0, 0, 2, 5), (4, 0, 2, 7), (0, 0, 1, 5), (3, 0, 1, 7), (0, 1, 0, 2), (2, 1, 0, 4),),
+    (5, 0): ((0, 1, 0, 1), (1, 1, 0, 3),),
+    (6, 0): ((0, 0, 1, 6), (0, 0, 2, 6), (0, 1, 1, 1), (0, 1, 1, 2), (3, 0, 3, 2), (4, 0, 3, 3), (1, 1, 2, 1), (2, 1, 2, 2),),
+    (7, 0, 1): ((0, 0, 2, 7),),
+    (7, 1, 1): ((0, 0, 1, 7), (0, 1, 0, 4), (3, 0, 3, 4), (4, 0, 3, 5), (2, 1, 0, 6),),
+    (7, 2, 0): ((0, 1, 0, 3), (1, 1, 0, 5),),
+    (7, 3, 1): ((0, 0, 3, 2), (0, 0, 3, 3), (0, 1, 2, 1), (0, 1, 2, 2), (3, 0, 3, 6), (4, 0, 3, 7), (1, 1, 2, 3), (2, 1, 2, 4),),
+    (7, 3, 2): ((0, 0, 3, 4), (0, 0, 3, 5), (0, 1, 0, 6), (3, 2, 1, 0), (4, 2, 2, 0), (2, 1, 1, 4), (0, 1, 0, 5), (1, 1, 0, 7),),
+    (7, 4, 2): ((0, 0, 3, 6), (0, 0, 3, 7), (0, 1, 2, 4), (2, 1, 2, 6), (0, 1, 2, 3), (1, 1, 2, 5),),
+    (7, 4, 3): ((0, 1, 3, 0),),
+    (7, 5, 1): ((0, 1, 0, 7), (0, 1, 1, 4), (1, 1, 3, 1), (2, 1, 3, 2),),
+    (7, 5, 3): ((0, 1, 2, 6), (2, 1, 1, 6), (0, 1, 2, 5), (1, 1, 2, 7),),
+    (7, 6, 2): ((0, 1, 3, 2), (2, 1, 3, 4), (0, 1, 3, 1), (1, 1, 3, 3),),
+    (7, 7, 1): ((0, 1, 1, 6), (0, 1, 2, 7), (2, 1, 1, 7), (1, 1, 1, 3),),
+    (7, 7, 3): ((0, 1, 3, 4), (2, 1, 3, 6), (0, 1, 3, 3), (1, 1, 3, 5),),
+    (7, 8, 2): ((0, 1, 1, 7), (0, 1, 1, 3), (1, 1, 1, 5),),
+    (7, 9, 2): ((0, 1, 3, 6), (2, 1, 3, 7), (0, 1, 3, 5),),
+    (7, 10, 0): ((0, 1, 1, 5),),
+    (7, 10, 3): ((0, 1, 3, 7),),
+}
+
 
 def kernel(
     wt, kw, q_hbm, k_hbm, v_hbm, ld, res_hbm, gain, tbl,
@@ -86,112 +119,6 @@
     ]
     for load in loads:
         load.start()
-    pl.semaphore_wait(barrier, len(peers))
-
-    def near(i):
-        half = lax.div(i + 1, 2)
-        return mod(z + half * (1 - 2 * lax.rem(i, 2)), NZ)
-
-    row_step = (0, 3, 1, 2)
-
-    def slot(r, i):
-        return at(mod(y + row_step[r], NY), near(i), c)
-
-    def w_rows(src, s, i):
-        send(src, gw.at[s], w_ys.at[0, i], w_r.at[1, i], up).start()
-        send(src, gw.at[s], w_ys.at[1, i], w_r.at[2, i], down).start()
-
-    def w_pass(src, s, r, i):
-        send(src, gw.at[s], w_ps.at[r, i], w_p.at[r, i], partner).start()
-
-    def w_start():
-        send(wt, gw.at[me], w_zs.at[0, 0], w_r.at[0, 1], ahead).start()
-        send(wt, gw.at[me], w_zs.at[1, 0], w_r.at[0, 2], behind).start()
-        w_rows(wt, me, 0)
-        w_pass(wt, me, 0, 0)
-
-    def w_along(i):
-        s = slot(0, i)
-        odd = lax.rem(i, 2)
-        arrive(gw.at[s], w_r.at[0, i])
-
-        @pl.when(i <= 5)
-        def _():
-            target = (at(y, mod(z + 2 * odd - 1, NZ), c), x)
-            send(
-                gw.at[s], gw.at[s], w_zs.at[1 - odd, lax.div(i + 1, 2)],
-                w_r.at[0, i + 2], target,
-            ).start()
-
-        w_rows(gw.at[s], s, i)
-        w_pass(gw.at[s], s, 0, i)
-
-    def w_across(i):
-        below, above = slot(1, i), slot(2, i)
-        even = lax.rem(i, 2) == 0
-        arrive(gw.at[below], w_r.at[1, i])
-        arrive(gw.at[above], w_r.at[2, i])
-        s = jnp.where(even, below, above)
-        target = (jnp.where(even, up[0], down[0]), x)
-        send(gw.at[s], gw.at[s], w_fs.at[i], w_r.at[3, i], target).start()
-        w_pass(gw.at[below], below, 1, i)
-        w_pass(gw.at[above], above, 2, i)
-
-    def w_last(i):
-        s = slot(3, i)
-        arrive(gw.at[s], w_r.at[3, i])
-        w_pass(gw.at[s], s, 3, i)
-
-    def k_along(src, s, r):
-        send(src, gk.at[s], k_zs.at[0, r, 0], k_r.at[r, 1], ahead).start()
-        send(src, gk.at[s], k_zs.at[1, r, 0], k_r.at[r, 2], behind).start()
-        send(src, gk.at[s], k_ps.at[r, 0], k_p.at[r, 0], partner).start()
-
-    def k_start():
-        send(kw, gk.at[me], k_ys.at[0], k_r.at[1, 0], up).start()
-        send(kw, gk.at[me], k_ys.at[1], k_r.at[2, 0], down).start()
-        k_along(kw, me, 0)
-
-    def k_across():
-        below, above = slot(1, 0), slot(2, 0)
-        arrive(gk.at[below], k_r.at[1, 0])
-        arrive(gk.at[above], k_r.at[2, 0])
-        low = gk.at[below, pl.ds(0, 32)]
-        top = gk.at[above, pl.ds(32, 32)]
-        send(low, low, k_fs.at[0], k_h.at[0], up).start()
-        send(top, top, k_fs.at[1], k_h.at[1], down).start()
-        k_along(gk.at[below], below, 1)
-        k_along(gk.at[above], above, 2)
-
-    def k_last():
-        s = slot(3, 0)
-        arrive(gk.at[s, pl.ds(0, 32)], k_h.at[0])
-        arrive(gk.at[s, pl.ds(32, 32)], k_h.at[1])
-        k_along(gk.at[s], s, 3)
-
-    def k_ring(i):
-        odd = lax.rem(i, 2)
-        for r in range(NY):
-            s = slot(r, i)
-            arrive(gk.at[s], k_r.at[r, i])
-
-            @pl.when(i <= 5)
-            def _():
-                target = (at(y, mod(z + 2 * odd - 1, NZ), c), x)
-                send(
-                    gk.at[s], gk.at[s], k_zs.at[1 - odd, r, lax.div(i + 1, 2)],
-                    k_r.at[r, i + 2], target,
-                ).start()
-
-            send(gk.at[s], gk.at[s], k_ps.at[r, i], k_p.at[r, i], partner).start()
-
-    w_start()
-    for n in range(2):
-        tb_s[n] = jnp.broadcast_to(tbl[0:1, n : n + 1], (8, HD))
-    for m in range(1, NX):
-        target = (me, mod(x + m, NX))
-        send(tb_s, tb.at[x], t_s.at[m - 1], t_r.at[m - 1], target).start()
-
     steps_a = lax.broadcasted_iota(jnp.int32, (BLK, BLK), 0)
     steps_b = lax.broadcasted_iota(jnp.int32, (BLK, BLK), 1)
     lower = jnp.where(steps_b <= steps_a, 1.0, 0.0).astype(F32)
@@ -204,6 +131,85 @@
         ccol[h] = wide
         a_s[h] = jnp.broadcast_to(wide[BLK - 1 : BLK, :], (8, HD))
 
+    pl.semaphore_wait(barrier, len(peers))
+
+    def near(i):
+        half = lax.div(i + 1, 2)
+        return mod(z + half * (1 - 2 * lax.rem(i, 2)), NZ)
+
+    row_step = (0, 3, 1, 2)
+
+    def slot(r, i):
+        return at(mod(y + row_step[r], NY), near(i), c)
+
+    lines = (None, ahead, behind, up, down)
+
+    def take(kind, r, i):
+        if kind == 0:
+            s = slot(r, i)
+            arrive(gw.at[s], w_r.at[r, i])
+            send(gw.at[s], gw.at[s], w_ps.at[r, i], w_p.at[r, i], partner).start()
+            return
+        s = slot(r, i)
+        if r == 3 and i == 0:
+            arrive(gk.at[s, pl.ds(0, 32)], k_h.at[0])
+            arrive(gk.at[s, pl.ds(32, 32)], k_h.at[1])
+        else:
+            arrive(gk.at[s], k_r.at[r, i])
+        send(gk.at[s], gk.at[s], k_ps.at[r, i], k_p.at[r, i], partner).start()
+
+    def along(i, link):
+        back = 0 if i <= 2 else (6 if i == 7 and link == 2 else i - 2)
+        index = (i - 1) // 2 if link == 1 else (3 if i == 7 else i // 2 - 1)
+        return back, index
+
+    def pass_on(link, kind, r, i):
+        target = lines[link]
+        if kind == 2:
+            s = slot(r, 0)
+            rows = gk.at[s, pl.ds(32 * (r - 1), 32)]
+            send(rows, rows, k_fs.at[r - 1], k_h.at[r - 1], target).start()
+            return
+        whole, mine = (gw, wt) if kind == 0 else (gk, kw)
+        if link <= 2:
+            back, index = along(i, link)
+            source = (r, back)
+            ssem = w_zs.at[link - 1, index] if kind == 0 else k_zs.at[link - 1, r, index]
+        elif kind == 1:
+            source, ssem = (0, 0), k_ys.at[link - 3]
+        elif r == 3:
+            source, ssem = (1 if link == 3 else 2, i), w_fs.at[i]
+        else:
+            source, ssem = (0, i), w_ys.at[link - 3, i]
+        s = slot(*source)
+        src = mine if source == (0, 0) else whole.at[s]
+        rsem = w_r.at[r, i] if kind == 0 else k_r.at[r, i]
+        send(src, whole.at[s], ssem, rsem, target).start()
+
+    def gather(*place):
+        for what, kind, r, i in PLAN.get(place, ()):
+            if what == 0:
+                take(kind, r, i)
+            else:
+                pass_on(what, kind, r, i)
+
+    def gather_at(step, steps, group, part):
+        for n in steps:
+            if (group, n, part) in PLAN:
+
+                @pl.when(step == n)
+                def _():
+                    gather(group, n, part)
+
+    send(wt, gw.at[me], w_ps.at[0, 0], w_p.at[0, 0], partner).start()
+    send(kw, gk.at[me], k_ps.at[0, 0], k_p.at[0, 0], partner).start()
+    gather(0, 0)
+    for n in range(2):
+        tb_s[n] = jnp.broadcast_to(tbl[0:1, n : n + 1], (8, HD))
+    for m in range(1, NX):
+        target = (me, mod(x + m, NX))
+        send(tb_s, tb.at[x], t_s.at[m - 1], t_r.at[m - 1], target).start()
+
     def head_cols(h):
         return pl.ds(pl.multiple_of(h * HD, HD), HD)
 
@@ -220,6 +226,7 @@
         return carry
 
     lax.fori_loop(0, HEADS, update, 0)
+    gather(1, 0)
     ub_s[...] = u_s[pl.ds(4 * (1 - c), 4)].astype(BF16)
     send(ub_s, ub_r, s1_s.at[0], s1_r.at[0], partner).start()
     send(a_s, a_r, s1_s.at[1], s1_r.at[1], partner).start()
@@ -237,30 +244,37 @@
             jnp.where(first, a_other, a_own),
         )
 
+    def split(row):
+        a = jnp.broadcast_to(row, (16, HD))
+        rows = lax.broadcasted_iota(jnp.int32, (16, HD), 0)
+        hi = a.astype(BF16).astype(F32)
+        mid = (a - hi).astype(BF16).astype(F32)
+        low = a - hi - mid
+        tile = jnp.where(rows == 0, hi, jnp.where(rows == 1, mid, jnp.where(rows == 2, low, 0.0)))
+        return tile.astype(BF16)
+
+    def joined(message):
+        value = message.astype(F32)
+        return value[0:64, :], jnp.sum(value[64:80, :], axis=0, keepdims=True)
+
     def scan_chip():
         arrive(ub_r, s1_r.at[0])
         arrive(a_r, s1_r.at[1])
         u0, u1, a0, a1 = chip_parts()
         total = jnp.exp(a1)[:, 0:1, :] * u0 + u1
         a_chip = a0 + a1
-        rows = lax.broadcasted_iota(jnp.int32, (16, HD), 0)
         for hl in range(4):
-            a = jnp.broadcast_to(a_chip[hl, 0:1, :], (16, HD))
-            hi = a.astype(BF16).astype(F32)
-            mid = (a - hi).astype(BF16).astype(F32)
-            low = a - hi - mid
-            tile = jnp.where(rows == 0, hi, jnp.where(rows == 1, mid, jnp.where(rows == 2, low, 0.0)))
+            tile = split(a_chip[hl, 0:1, :])
             for half in range(2):
                 st_s[2 * hl + half, 0:64, :] = total[hl, 64 * half : 64 * half + 64, :].astype(BF16)
-                st_s[2 * hl + half, 64:80, :] = tile.astype(BF16)
+                st_s[2 * hl + half, 64:80, :] = tile
         st_r[z] = st_s[z]
         for m in range(1, NZ):
             zz = mod(z + m, NZ)
             send(st_s.at[zz], st_r.at[z], s2_s.at[m], s2_r.at[m], (at(y, zz, c), x)).start()
 
     def chip_total(zz):
-        message = st_r[zz].astype(F32)
-        return message[0:64, :], jnp.sum(message[64:80, :], axis=0, keepdims=True)
+        return joined(st_r[zz])
 
     def scan_row():
         for m in range(1, NZ):
@@ -271,8 +285,8 @@
             t, a = chip_total(zz)
             total = jnp.exp(a) * total + t
             a_row = a_row + a
-        sr_s[0:64, :] = total
-        sr_s[64:72, :] = jnp.broadcast_to(a_row, (8, HD))
+        sr_s[0:64, :] = total.astype(BF16)
+        sr_s[64:80, :] = split(a_row)
         sr_r[y] = sr_s[...]
         for m in range(1, NY):
             target = (at(mod(y + m, NY), z, c), x)
@@ -283,7 +297,8 @@
             arrive(sr_r.at[mod(y - m, NY)], s3_r.at[m])
         enter = jnp.zeros((64, HD), F32)
         for yy in range(NY):
-            moved = jnp.exp(sr_r[yy, 64:65, :]) * enter + sr_r[yy, 0:64, :]
+            t, a = joined(sr_r[yy])
+            moved = jnp.exp(a) * enter + t
             enter = jnp.where(yy < y, moved, enter)
         for zz in range(NZ):
             se_s[zz] = enter.astype(BF16)
@@ -314,21 +329,17 @@
     seen = tri_b <= tri_a
 
     def within(h, carry):
+        gather_at(h, range(HEADS), 2, 0)
+
         @pl.when(h == 1)
         def _():
             scan_chip()
 
-        @pl.when(h == 4)
+        @pl.when(h == 5)
         def _():
             scan_row()
 
-        @pl.when(h == 5)
-        def _():
-            k_start()
-
-        @pl.when(h == 6)
-        def _():
-            scan_back()
+        gather_at(h, range(HEADS), 2, 1)
 
         for tq in range(4):
             rows = pl.ds(tq * HD, HD)
@@ -351,17 +362,19 @@
                 scores, v_s[0:width, head_cols(h)], preferred_element_type=F32
             )
 
-        @pl.when(h >= 1)
-        def _():
-            w_along(h)
-
+        gather_at(h, range(HEADS), 2, 2)
         return carry
 
     lax.fori_loop(0, HEADS, within, 0)
+    gather(3, 0)
+    scan_back()
+    gather(3, 1)
+    gather(4, 0)
     scan_cores()
-    w_across(0)
-    w_across(1)
+    gather(4, 1)
+    gather(5, 0)
     arrive(sf_r, s5_r.at[0])
+    gather(5, 1)
     state[pl.ds(4 * (1 - c), 4)] = sf_r[...]
 
     def finish(h, carry):
@@ -373,6 +386,7 @@
 
     lax.fori_loop(0, HEADS, finish, 0)
     loads[3].wait()
+    gather(6, 0)
 
     def row_of(r):
         step = jnp.where(r == 1, 3, jnp.where(r == 2, 1, jnp.where(r == 3, 2, 0)))
@@ -397,9 +411,13 @@
             arrive(gw.at[s], w_p.at[r, i])
 
     def reduce(t, carry):
-        @pl.when(t == 0)
-        def _():
-            w_ready(0)
+        steps = range(CH + 4)
+        gather_at(t, steps, 7, 0)
+        for r in range(NY):
+
+            @pl.when(t == 2 * r)
+            def _():
+                w_ready(r)
 
         @pl.when(t < CH)
         def _():
@@ -410,59 +428,33 @@
                 block = mod(x + direction(d)[1], NX)
                 forward(t, 0, d, part[t, block, :, d * DW : d * DW + DW])
 
+        gather_at(t, steps, 7, 1)
         for step in (1, 2):
 
-            @pl.when(jnp.logical_and(t >= step, t < CH + step))
+            @pl.when(jnp.logical_and(t >= step + 1, t < CH + step + 1))
             def _():
-                j = t - step
+                j = t - step - 1
                 for d in range(2):
                     arrive(rs_r.at[d, j, step - 1], rs_rs.at[d, j, step - 1])
                     block = lax.rem(x + direction(d)[1] * (1 + step) + 2 * NX, NX)
                     own = part[j, block, :, d * DW : d * DW + DW]
                     forward(j, step, d, rs_r[d, j, step - 1].astype(F32) + own)
 
-        @pl.when(t >= 3)
+            gather_at(t, steps, 7, step + 1)
+
+        @pl.when(t >= 4)
         def _():
-            j = t - 3
+            j = t - 4
             for d in range(2):
                 arrive(rs_r.at[d, j, 2], rs_rs.at[d, j, 2])
                 own = part[j, x, :, d * DW : d * DW + DW]
                 cols = pl.ds(pl.multiple_of(chunk_rows(j) * 64 + d * DW, DW), DW)
                 hid[:, cols] = rs_r[d, j, 2].astype(F32) + own + res_s[:, cols].astype(F32)
 
-        @pl.when(t == 0)
-        def _():
-            k_across()
-            for i in (2, 3, 4):
-                w_across(i)
-
-        @pl.when(t == 1)
-        def _():
-            k_last()
-            for i in (5, 6, 7):
-                w_across(i)
-            w_ready(1)
-
-        @pl.when(jnp.logical_and(t >= 2, t < 4))
-        def _():
-            for i in range(4):
-                w_last(4 * (t - 2) + i)
-
-        @pl.when(t == 3)
-        def _():
-            w_ready(2)
-
-        @pl.when(t == 5)
-        def _():
-            w_ready(3)
-
-        @pl.when(jnp.logical_and(t >= 2, t < 9))
-        def _():
-            k_ring(t - 1)
-
-        return carry
-
-    lax.fori_loop(0, CH + 3, reduce, 0)
+        gather_at(t, steps, 7, 4)
+        return carry
+
+    lax.fori_loop(0, CH + 4, reduce, 0)
 
     def square(j, total):
         cols = pl.ds(pl.multiple_of(j * CW, CW), CW)
@@ -478,6 +470,9 @@
         return carry
 
     lax.fori_loop(0, CH, normalize, 0)
+
+    gather(8, 0)
+    gather(9, 0)
 
     def k_ready(i, carry):
         for r in range(NY):
@@ -528,11 +523,13 @@
         return carry
 
     lax.fori_loop(0, NZ, drain_w, 0)
-    for d, count in ((0, 4), (1, 3)):
-        for n in range(count):
-            sent(gw.at[0], w_zs.at[d, n])
+    for n in range(4):
+        for d in range(2):
+            if n < 3 or d == 1:
+                sent(gw.at[0], w_zs.at[d, n])
             for r in range(NY):
-                sent(gk.at[0], k_zs.at[d, r, n])
+                if n < 3 or d == r % 2:
+                    sent(gk.at[0], k_zs.at[d, r, n])
     for d in range(2):
         sent(gk.at[0], k_ys.at[d])
         sent(gk.at[0, pl.ds(0, 32)], k_fs.at[d])
@@ -599,8 +596,8 @@
             vm((4, HD, HD), BF16),
             vm((NZ, 80, HD), BF16),
             vm((NZ, 80, HD), BF16),
-            vm((72, HD), F32),
-            vm((NY, 72, HD), F32),
+            vm((80, HD), BF16),
+            vm((NY, 80, HD), BF16),
             vm((NZ, 64, HD), BF16),
             vm((NZ, 64, HD), BF16),
             vm((4, HD, HD), BF16),

time: 113 us -> 102 us (0.903)
  Pallas kernels: 111 us -> 99.3 us
    pallas_call x1, Pallas kernels: 111 us -> 99.3 us  [on_device(): pl.pallas_call(kernel, out_shape=jax.ShapeDtypeStruct((2, PAGE, KVW), BF1...]
where the time goes in v3:
time: 102 us; the launch traced here: 101 us
  Pallas kernels  99.3 us (97%)
  local copies, waits for them, and re-layouts  1.87 us (2%)
    pallas_call x1, Pallas kernels, on_device(): pl.pallas_call(kernel, out_shape=jax.ShapeDtypeStruct((2, PAGE, KVW), BF1...  99.3 us

profile of v3, /device:TPU:6, one launch (start us, length us, event | category | flops | bytes accessed | tf_op | source)
XLA Modules:
  0.0 101.2 jit_solution(17717889500566738356)
XLA Ops:
  0.0 99.3 %layer.1 = bf16[2,128,1024]{2,1,0:T(8,128)(2,1)} custom-call(bf16[64,1024]{1,0:T(8,128)(2,1)} %bitcast.4, bf16[64,1024]{1,0:T(8,128)(2,1)} %kw.1, bf16[512,1024]{1,0:T(8,128)(2,1)} %q_hbm.1, bf16[512,1024]{1,0:T(8,128)(2,1)} %k_hbm.1, bf16[512,1024]{1,0:T(8,128)(2,1)} %v_hbm.1, f32[8,512]{1,0:T(8,128)} %ld.1, bf16[128,4096]{1,0:T(8,128)(2,1)} %res_hbm.1, ...), custom_call_target="tpu_custom_call" | custom-call | tf_op jit(solution)/shard_map/layer/pallas_call | solution.py:576
  99.3 1.9 %copy.11 = bf16[1,1,2,128,1024]{4,3,2,1,0:T(8,128)(2,1)} copy(bf16[1,1,2,128,1024]{4,3,2,1,0:T(8,128)(2,1)} %bitcast.3) | data formatting | bytes 1048576

commit v4 on v3

--- a/solution.py
+++ b/solution.py
@@ -20,41 +20,47 @@
 F32 = jnp.float32
 BF16 = jnp.bfloat16
 MESH = pl.DeviceIdType.MESH
+FAR_Z = (4, 3, 5, 2, 6, 1, 7)
 NT_DIMS = (((1,), (1,)), ((), ()))
 TN_DIMS = (((0,), (0,)), ((), ()))
-HIGH = lax.Precision.HIGHEST
 
 PLAN = {
     (0, 0): ((1, 0, 0, 1), (2, 0, 0, 2), (3, 0, 1, 0), (4, 0, 2, 0),),
     (1, 0): ((3, 1, 1, 0), (4, 1, 2, 0),),
-    (2, 1, 1): ((0, 0, 0, 1), (0, 0, 0, 2), (0, 0, 1, 0), (0, 0, 2, 0), (3, 0, 1, 1), (4, 0, 2, 1),),
-    (2, 2, 2): ((2, 0, 0, 4),),
-    (2, 4, 2): ((0, 1, 1, 0), (0, 1, 2, 0), (3, 0, 1, 2), (4, 0, 2, 2), (1, 0, 0, 3),),
-    (2, 5, 0): ((0, 0, 1, 1), (0, 0, 2, 1), (3, 0, 3, 0), (4, 0, 3, 1), (0, 0, 0, 4), (2, 0, 0, 6),),
-    (2, 5, 1): ((0, 0, 1, 2), (0, 0, 2, 2),),
-    (2, 5, 2): ((0, 0, 0, 3), (1, 0, 0, 5), (4, 0, 2, 3),),
-    (2, 6, 2): ((3, 0, 1, 3),),
-    (2, 7, 2): ((0, 0, 3, 0), (0, 0, 3, 1),),
-    (3, 0): ((0, 0, 0, 6), (2, 0, 0, 7), (4, 0, 2, 4), (3, 0, 1, 4),),
-    (4, 0): ((0, 0, 0, 5), (0, 0, 2, 3), (4, 0, 2, 5), (0, 0, 1, 3), (3, 0, 1, 5), (2, 1, 0, 2), (0, 0, 0, 7), (1, 1, 0, 1), (0, 0, 2, 4), (4, 0, 2, 6), (0, 0, 1, 4), (3, 0, 1, 6), (2, 1, 1, 2), (1, 1, 1, 1), (0, 0, 2, 5), (4, 0, 2, 7), (0, 0, 1, 5), (3, 0, 1, 7), (0, 1, 0, 2), (2, 1, 0, 4),),
-    (5, 0): ((0, 1, 0, 1), (1, 1, 0, 3),),
-    (6, 0): ((0, 0, 1, 6), (0, 0, 2, 6), (0, 1, 1, 1), (0, 1, 1, 2), (3, 0, 3, 2), (4, 0, 3, 3), (1, 1, 2, 1), (2, 1, 2, 2),),
-    (7, 0, 1): ((0, 0, 2, 7),),
-    (7, 1, 1): ((0, 0, 1, 7), (0, 1, 0, 4), (3, 0, 3, 4), (4, 0, 3, 5), (2, 1, 0, 6),),
-    (7, 2, 0): ((0, 1, 0, 3), (1, 1, 0, 5),),
-    (7, 3, 1): ((0, 0, 3, 2), (0, 0, 3, 3), (0, 1, 2, 1), (0, 1, 2, 2), (3, 0, 3, 6), (4, 0, 3, 7), (1, 1, 2, 3), (2, 1, 2, 4),),
-    (7, 3, 2): ((0, 0, 3, 4), (0, 0, 3, 5), (0, 1, 0, 6), (3, 2, 1, 0), (4, 2, 2, 0), (2, 1, 1, 4), (0, 1, 0, 5), (1, 1, 0, 7),),
-    (7, 4, 2): ((0, 0, 3, 6), (0, 0, 3, 7), (0, 1, 2, 4), (2, 1, 2, 6), (0, 1, 2, 3), (1, 1, 2, 5),),
-    (7, 4, 3): ((0, 1, 3, 0),),
-    (7, 5, 1): ((0, 1, 0, 7), (0, 1, 1, 4), (1, 1, 3, 1), (2, 1, 3, 2),),
-    (7, 5, 3): ((0, 1, 2, 6), (2, 1, 1, 6), (0, 1, 2, 5), (1, 1, 2, 7),),
-    (7, 6, 2): ((0, 1, 3, 2), (2, 1, 3, 4), (0, 1, 3, 1), (1, 1, 3, 3),),
-    (7, 7, 1): ((0, 1, 1, 6), (0, 1, 2, 7), (2, 1, 1, 7), (1, 1, 1, 3),),
-    (7, 7, 3): ((0, 1, 3, 4), (2, 1, 3, 6), (0, 1, 3, 3), (1, 1, 3, 5),),
-    (7, 8, 2): ((0, 1, 1, 7), (0, 1, 1, 3), (1, 1, 1, 5),),
-    (7, 9, 2): ((0, 1, 3, 6), (2, 1, 3, 7), (0, 1, 3, 5),),
-    (7, 10, 0): ((0, 1, 1, 5),),
-    (7, 10, 3): ((0, 1, 3, 7),),
+    (2, 2, 2): ((0, 0, 0, 1), (0, 0, 0, 2), (0, 0, 1, 0), (0, 0, 2, 0), (2, 0, 0, 4), (3, 0, 1, 1), (4, 0, 2, 1),),
+    (2, 5, 0): ((1, 0, 0, 3), (3, 0, 1, 2), (4, 0, 2, 2), (0, 1, 1, 0), (0, 1, 2, 0),),
+    (2, 5, 1): ((4, 2, 2, 0),),
+    (2, 5, 2): ((0, 0, 1, 1), (0, 0, 2, 1), (3, 2, 1, 0),),
+    (2, 6, 2): ((0, 0, 0, 4), (2, 0, 0, 6), (4, 0, 2, 4),),
+    (2, 7, 0): ((3, 0, 1, 4), (0, 0, 0, 3), (1, 0, 0, 5), (0, 0, 1, 2), (0, 0, 2, 2),),
+    (2, 7, 1): ((4, 0, 2, 3),),
+    (2, 7, 2): ((3, 0, 1, 3),),
+    (4, 0): ((2, 1, 1, 2), (0, 1, 3, 0), (4, 0, 3, 1), (0, 0, 0, 6), (0, 0, 2, 4), (3, 0, 1, 6), (1, 1, 1, 1), (2, 0, 0, 7), (0, 0, 0, 5), (0, 0, 1, 4), (4, 0, 2, 5), (0, 0, 2, 3), (3, 0, 1, 5), (1, 1, 0, 1), (2, 1, 0, 2),),
+    (4, 1): ((0, 0, 1, 3),),
+    (5, 0): ((0, 1, 1, 2), (4, 0, 2, 6),),
+    (6, 0): ((0, 0, 0, 7), (0, 0, 3, 1), (0, 0, 1, 6), (0, 1, 1, 1), (3, 0, 1, 7), (1, 1, 2, 1), (2, 1, 2, 2),),
+    (7, 0, 0): ((4, 0, 2, 7),),
+    (7, 0, 1): ((0, 0, 2, 5), (3, 0, 3, 0), (1, 1, 3, 1), (2, 1, 3, 2),),
+    (7, 1, 1): ((0, 0, 1, 5), (0, 1, 0, 1), (0, 1, 0, 2),),
+    (7, 2, 0): ((4, 0, 3, 3), (0, 0, 2, 6), (3, 0, 3, 2), (1, 1, 0, 3), (2, 1, 1, 4), (0, 0, 1, 7), (0, 1, 2, 1), (0, 1, 2, 2), (4, 0, 3, 5),),
+    (7, 2, 1): ((0, 0, 2, 7), (3, 0, 3, 4), (1, 1, 2, 3), (2, 1, 2, 4),),
+    (7, 3, 1): ((0, 0, 3, 0), (0, 1, 3, 1), (0, 1, 3, 2), (4, 0, 3, 7),),
+    (7, 3, 2): ((0, 0, 3, 3), (3, 0, 3, 6), (1, 1, 3, 3), (2, 1, 3, 4), (0, 0, 3, 2), (0, 1, 0, 3), (0, 1, 1, 4),),
+    (7, 4, 1): ((0, 0, 3, 5), (1, 1, 0, 5), (2, 1, 1, 6),),
+    (7, 4, 2): ((0, 0, 3, 4), (0, 1, 2, 3), (0, 1, 2, 4),),
+    (7, 4, 3): ((0, 0, 3, 7), (1, 1, 2, 5), (2, 1, 2, 6),),
+    (7, 5, 1): ((0, 0, 3, 6), (0, 1, 3, 3), (0, 1, 3, 4),),
+    (7, 5, 2): ((1, 1, 3, 5), (2, 1, 3, 6),),
+    (7, 5, 3): ((0, 1, 0, 5), (0, 1, 1, 6),),
+    (7, 6, 2): ((1, 1, 0, 7), (2, 1, 1, 7), (0, 1, 2, 5), (0, 1, 2, 6),),
+    (7, 6, 3): ((1, 1, 2, 7), (2, 1, 0, 4),),
+    (7, 7, 1): ((0, 1, 3, 5), (0, 1, 3, 6),),
+    (7, 7, 2): ((1, 1, 1, 3), (2, 1, 3, 7),),
+    (7, 7, 3): ((0, 1, 0, 7), (0, 1, 1, 7),),
+    (7, 8, 2): ((0, 1, 2, 7), (0, 1, 0, 4), (2, 1, 0, 6),),
+    (7, 9, 2): ((0, 1, 1, 3), (0, 1, 3, 7), (1, 1, 1, 5),),
+    (7, 10, 0): ((0, 1, 0, 6),),
+    (7, 11, 0): ((0, 1, 1, 5),),
 }
 
 
@@ -63,7 +69,7 @@
     cache,
     gw, gk, q_s, k_s, v_s, res_s, crow, ccol, a_s, a_r, u_s, inner, mixed,
     ub_s, ub_r, st_s, st_r, sr_s, sr_r, se_s, se_r, sf_s, sf_r, state,
-    part, rs_s, rs_r, hid, norm, pg, tb, tb_s,
+    part, rs_s, rs_r, squares, norm, pg, tb, tb_s,
     ld_sem, w_zs, w_ys, w_fs, w_ps, w_r, w_p,
     k_zs, k_ys, k_fs, k_ps, k_r, k_h, k_p,
     s1_s, s1_r, s2_s, s2_r, s3_s, s3_r, s4_s, s4_r, s5_s, s5_r,
@@ -121,10 +127,15 @@
         load.start()
     steps_a = lax.broadcasted_iota(jnp.int32, (BLK, BLK), 0)
     steps_b = lax.broadcasted_iota(jnp.int32, (BLK, BLK), 1)
-    lower = jnp.where(steps_b <= steps_a, 1.0, 0.0).astype(F32)
-    decay = ld[...]
-    sums_row = lax.dot_general(decay, lower, NT_DIMS, precision=HIGH, preferred_element_type=F32)
-    sums_col = lax.dot_general(lower, decay, NT_DIMS, precision=HIGH, preferred_element_type=F32)
+    lower = jnp.where(steps_b <= steps_a, 1.0, 0.0).astype(BF16)
+    rest = ld[...]
+    sums_row = jnp.zeros((HEADS, BLK), F32)
+    sums_col = jnp.zeros((BLK, HEADS), F32)
+    for _ in range(3):
+        piece = rest.astype(BF16)
+        rest = rest - piece.astype(F32)
+        sums_row += lax.dot_general(piece, lower, NT_DIMS, preferred_element_type=F32)
+        sums_col += lax.dot_general(lower, piece, NT_DIMS, preferred_element_type=F32)
     for h in range(HEADS):
         crow[h] = sums_row[h : h + 1, :]
         wide = jnp.broadcast_to(sums_col[:, h : h + 1], (BLK, HD))
@@ -269,7 +280,7 @@
                 st_s[2 * hl + half, 0:64, :] = total[hl, 64 * half : 64 * half + 64, :].astype(BF16)
                 st_s[2 * hl + half, 64:80, :] = tile
         st_r[z] = st_s[z]
-        for m in range(1, NZ):
+        for m in FAR_Z:
             zz = mod(z + m, NZ)
             send(st_s.at[zz], st_r.at[z], s2_s.at[m], s2_r.at[m], (at(y, zz, c), x)).start()
 
@@ -288,7 +299,7 @@
         sr_s[0:64, :] = total.astype(BF16)
         sr_s[64:80, :] = split(a_row)
         sr_r[y] = sr_s[...]
-        for m in range(1, NY):
+        for m in (2, 1, 3):
             target = (at(mod(y + m, NY), z, c), x)
             send(sr_s, sr_r.at[y], s3_s.at[m], s3_r.at[m], target).start()
 
@@ -305,7 +316,7 @@
             t, a = chip_total(zz)
             enter = jnp.exp(a) * enter + t
         se_r[z] = se_s[z]
-        for m in range(1, NZ):
+        for m in FAR_Z:
             zz = mod(z + m, NZ)
             send(se_s.at[zz], se_r.at[z], s4_s.at[m], s4_r.at[m], (at(y, zz, c), x)).start()
 
@@ -338,6 +349,10 @@
         @pl.when(h == 5)
         def _():
             scan_row()
+
+        @pl.when(h == 7)
+        def _():
+            scan_back()
 
         gather_at(h, range(HEADS), 2, 1)
 
@@ -362,13 +377,11 @@
                 scores, v_s[0:width, head_cols(h)], preferred_element_type=F32
             )
 
+        ccol[h] = jnp.exp(ccol[h])
         gather_at(h, range(HEADS), 2, 2)
         return carry
 
     lax.fori_loop(0, HEADS, within, 0)
-    gather(3, 0)
-    scan_back()
-    gather(3, 1)
     gather(4, 0)
     scan_cores()
     gather(4, 1)
@@ -379,7 +392,7 @@
 
     def finish(h, carry):
         outer = jnp.dot(q_s[:, head_cols(h)], state[h], preferred_element_type=F32)
-        kept = inner[:, head_cols(h)] + outer * jnp.exp(ccol[h])
+        kept = inner[:, head_cols(h)] + outer * ccol[h]
         scale = lax.rsqrt(jnp.mean(kept * kept, axis=-1, keepdims=True) + 1e-05)
         mixed[:, head_cols(h)] = (kept * scale).astype(BF16)
         return carry
@@ -449,28 +462,18 @@
                 arrive(rs_r.at[d, j, 2], rs_rs.at[d, j, 2])
                 own = part[j, x, :, d * DW : d * DW + DW]
                 cols = pl.ds(pl.multiple_of(chunk_rows(j) * 64 + d * DW, DW), DW)
-                hid[:, cols] = rs_r[d, j, 2].astype(F32) + own + res_s[:, cols].astype(F32)
+                hidden = rs_r[d, j, 2].astype(F32) + own + res_s[:, cols].astype(F32)
+                norm[:, cols] = (hidden * gain[:, cols]).astype(BF16)
+                square = hidden * hidden
+                squares[...] += square[:, :HD] + square[:, HD:]
 
         gather_at(t, steps, 7, 4)
         return carry
 
+    squares[...] = jnp.zeros_like(squares)
     lax.fori_loop(0, CH + 4, reduce, 0)
 
-    def square(j, total):
-        cols = pl.ds(pl.multiple_of(j * CW, CW), CW)
-        value = hid[:, cols]
-        return total + jnp.sum(value * value, axis=-1, keepdims=True)
-
-    squares = lax.fori_loop(0, CH, square, jnp.zeros((PAGE, 1), F32))
-    scale = lax.rsqrt(squares * (1.0 / D) + 1e-05)
-
-    def normalize(j, carry):
-        cols = pl.ds(pl.multiple_of(j * CW, CW), CW)
-        norm[:, cols] = (hid[:, cols] * scale * gain[:, cols]).astype(BF16)
-        return carry
-
-    lax.fori_loop(0, CH, normalize, 0)
-
+    scale = lax.rsqrt(jnp.sum(squares[...], axis=-1, keepdims=True) * (1.0 / D) + 1e-05)
     gather(8, 0)
     gather(9, 0)
 
@@ -493,7 +496,7 @@
         def _():
             weight = gk[:, :, tile(n)].reshape(D, TW)
             value = jnp.dot(norm[...], weight, preferred_element_type=F32)
-            pg[x, :, tile(n)] = value.astype(BF16)
+            pg[x, :, tile(n)] = (value * scale).astype(BF16)
             own = pg.at[x, :, tile(n)]
             send(own, own, g_s.at[0, n], g_r.at[0, n], right).start()
             send(own, own, g_s.at[1, n], g_r.at[1, n], left).start()
@@ -606,7 +609,7 @@
             vm((CH, NX, PAGE, CW), F32),
             vm((2, CH, 3, PAGE, DW), BF16),
             vm((2, CH, 3, PAGE, DW), BF16),
-            vm((PAGE, D), F32),
+            vm((PAGE, HD), F32),
             vm((PAGE, D), BF16),
             vm((NX, PAGE, KVW), BF16),
             vm((NX, 2, 8, HD), jnp.int32),

time: 102 us -> 98.8 us (0.969)
  Pallas kernels: 99.3 us -> 96.7 us
    pallas_call x1, Pallas kernels: 99.3 us -> 96.7 us  [on_device(): pl.pallas_call(kernel, out_shape=jax.ShapeDtypeStruct((2, PAGE, KVW), BF1...]
where the time goes in v4:
time: 98.8 us; the launch traced here: 98.6 us
  Pallas kernels  96.7 us (98%)
  local copies, waits for them, and re-layouts  1.87 us (2%)
    pallas_call x1, Pallas kernels, on_device(): pl.pallas_call(kernel, out_shape=jax.ShapeDtypeStruct((2, PAGE, KVW), BF1...  96.7 us

profile of v4, /device:TPU:6, one launch (start us, length us, event | category | flops | bytes accessed | tf_op | source)
XLA Modules:
  0.0 98.6 jit_solution(14772629310825717403)
XLA Ops:
  0.0 96.7 %layer.1 = bf16[2,128,1024]{2,1,0:T(8,128)(2,1)} custom-call(bf16[64,1024]{1,0:T(8,128)(2,1)} %bitcast.4, bf16[64,1024]{1,0:T(8,128)(2,1)} %kw.1, bf16[512,1024]{1,0:T(8,128)(2,1)} %q_hbm.1, bf16[512,1024]{1,0:T(8,128)(2,1)} %k_hbm.1, bf16[512,1024]{1,0:T(8,128)(2,1)} %v_hbm.1, f32[8,512]{1,0:T(8,128)} %ld.1, bf16[128,4096]{1,0:T(8,128)(2,1)} %res_hbm.1, ...), custom_call_target="tpu_custom_call" | custom-call | tf_op jit(solution)/shard_map/layer/pallas_call | solution.py:579
  96.7 1.9 %copy.11 = bf16[1,1,2,128,1024]{4,3,2,1,0:T(8,128)(2,1)} copy(bf16[1,1,2,128,1024]{4,3,2,1,0:T(8,128)(2,1)} %bitcast.3) | data formatting | bytes 1048576

commit v5 on v4

--- a/solution.py
+++ b/solution.py
@@ -15,6 +15,7 @@
 CH = 8
 CW = D // CH
 DW = CW // 2
+LAGS = (2, 4, 6)
 NT = 4
 TW = KVW // NT
 F32 = jnp.float32
@@ -45,22 +46,23 @@
     (7, 2, 0): ((4, 0, 3, 3), (0, 0, 2, 6), (3, 0, 3, 2), (1, 1, 0, 3), (2, 1, 1, 4), (0, 0, 1, 7), (0, 1, 2, 1), (0, 1, 2, 2), (4, 0, 3, 5),),
     (7, 2, 1): ((0, 0, 2, 7), (3, 0, 3, 4), (1, 1, 2, 3), (2, 1, 2, 4),),
     (7, 3, 1): ((0, 0, 3, 0), (0, 1, 3, 1), (0, 1, 3, 2), (4, 0, 3, 7),),
-    (7, 3, 2): ((0, 0, 3, 3), (3, 0, 3, 6), (1, 1, 3, 3), (2, 1, 3, 4), (0, 0, 3, 2), (0, 1, 0, 3), (0, 1, 1, 4),),
-    (7, 4, 1): ((0, 0, 3, 5), (1, 1, 0, 5), (2, 1, 1, 6),),
-    (7, 4, 2): ((0, 0, 3, 4), (0, 1, 2, 3), (0, 1, 2, 4),),
-    (7, 4, 3): ((0, 0, 3, 7), (1, 1, 2, 5), (2, 1, 2, 6),),
-    (7, 5, 1): ((0, 0, 3, 6), (0, 1, 3, 3), (0, 1, 3, 4),),
-    (7, 5, 2): ((1, 1, 3, 5), (2, 1, 3, 6),),
-    (7, 5, 3): ((0, 1, 0, 5), (0, 1, 1, 6),),
-    (7, 6, 2): ((1, 1, 0, 7), (2, 1, 1, 7), (0, 1, 2, 5), (0, 1, 2, 6),),
-    (7, 6, 3): ((1, 1, 2, 7), (2, 1, 0, 4),),
-    (7, 7, 1): ((0, 1, 3, 5), (0, 1, 3, 6),),
-    (7, 7, 2): ((1, 1, 1, 3), (2, 1, 3, 7),),
-    (7, 7, 3): ((0, 1, 0, 7), (0, 1, 1, 7),),
-    (7, 8, 2): ((0, 1, 2, 7), (0, 1, 0, 4), (2, 1, 0, 6),),
-    (7, 9, 2): ((0, 1, 1, 3), (0, 1, 3, 7), (1, 1, 1, 5),),
-    (7, 10, 0): ((0, 1, 0, 6),),
-    (7, 11, 0): ((0, 1, 1, 5),),
+    (7, 4, 1): ((0, 0, 3, 3), (3, 0, 3, 6), (1, 1, 3, 3), (2, 1, 3, 4),),
+    (7, 4, 2): ((0, 0, 3, 2), (0, 1, 0, 3), (0, 1, 1, 4),),
+    (7, 5, 1): ((0, 0, 3, 5), (1, 1, 0, 5), (2, 1, 1, 6),),
+    (7, 5, 2): ((0, 0, 3, 4), (0, 1, 2, 3), (0, 1, 2, 4),),
+    (7, 6, 0): ((0, 0, 3, 7), (1, 1, 2, 5), (2, 1, 2, 6), (0, 0, 3, 6), (0, 1, 3, 3), (0, 1, 3, 4),),
+    (7, 6, 2): ((1, 1, 3, 5), (2, 1, 3, 6),),
+    (7, 7, 1): ((0, 1, 0, 5), (0, 1, 1, 6),),
+    (7, 7, 2): ((1, 1, 0, 7), (2, 1, 1, 7),),
+    (7, 7, 3): ((0, 1, 2, 5), (0, 1, 2, 6),),
+    (7, 8, 0): ((1, 1, 2, 7), (2, 1, 0, 4),),
+    (7, 8, 2): ((0, 1, 3, 5), (0, 1, 3, 6),),
+    (7, 8, 3): ((1, 1, 1, 3), (2, 1, 3, 7),),
+    (7, 9, 0): ((0, 1, 0, 7), (0, 1, 1, 7),),
+    (7, 9, 3): ((0, 1, 2, 7), (0, 1, 0, 4), (2, 1, 0, 6),),
+    (7, 10, 3): ((0, 1, 1, 3), (0, 1, 3, 7), (1, 1, 1, 5),),
+    (7, 11, 3): ((0, 1, 0, 6),),
+    (7, 13, 0): ((0, 1, 1, 5),),
 }
 
 
@@ -424,7 +426,7 @@
             arrive(gw.at[s], w_p.at[r, i])
 
     def reduce(t, carry):
-        steps = range(CH + 4)
+        steps = range(CH + LAGS[2])
         gather_at(t, steps, 7, 0)
         for r in range(NY):
 
@@ -444,9 +446,11 @@
         gather_at(t, steps, 7, 1)
         for step in (1, 2):
 
-            @pl.when(jnp.logical_and(t >= step + 1, t < CH + step + 1))
+            lag = LAGS[step - 1]
+
+            @pl.when(jnp.logical_and(t >= lag, t < CH + lag))
             def _():
-                j = t - step - 1
+                j = t - lag
                 for d in range(2):
                     arrive(rs_r.at[d, j, step - 1], rs_rs.at[d, j, step - 1])
                     block = lax.rem(x + direction(d)[1] * (1 + step) + 2 * NX, NX)
@@ -455,9 +459,9 @@
 
             gather_at(t, steps, 7, step + 1)
 
-        @pl.when(t >= 4)
+        @pl.when(t >= LAGS[2])
         def _():
-            j = t - 4
+            j = t - LAGS[2]
             for d in range(2):
                 arrive(rs_r.at[d, j, 2], rs_rs.at[d, j, 2])
                 own = part[j, x, :, d * DW : d * DW + DW]
@@ -471,7 +475,7 @@
         return carry
 
     squares[...] = jnp.zeros_like(squares)
-    lax.fori_loop(0, CH + 4, reduce, 0)
+    lax.fori_loop(0, CH + LAGS[2], reduce, 0)
 
     scale = lax.rsqrt(jnp.sum(squares[...], axis=-1, keepdims=True) * (1.0 / D) + 1e-05)
     gather(8, 0)

time: 98.8 us -> 97 us (0.982)
  Pallas kernels: 96.7 us -> 94.9 us
    pallas_call x1, Pallas kernels: 96.7 us -> 94.9 us  [on_device(): pl.pallas_call(kernel, out_shape=jax.ShapeDtypeStruct((2, PAGE, KVW), BF1...]
where the time goes in v5:
time: 97 us; the launch traced here: 96.8 us
  Pallas kernels  94.9 us (98%)
  local copies, waits for them, and re-layouts  1.87 us (2%)
    pallas_call x1, Pallas kernels, on_device(): pl.pallas_call(kernel, out_shape=jax.ShapeDtypeStruct((2, PAGE, KVW), BF1...  94.9 us

profile of v5, /device:TPU:6, one launch (start us, length us, event | category | flops | bytes accessed | tf_op | source)
XLA Modules:
  0.0 96.8 jit_solution(16411894536097357233)
XLA Ops:
  0.0 94.9 %layer.1 = bf16[2,128,1024]{2,1,0:T(8,128)(2,1)} custom-call(bf16[64,1024]{1,0:T(8,128)(2,1)} %bitcast.4, bf16[64,1024]{1,0:T(8,128)(2,1)} %kw.1, bf16[512,1024]{1,0:T(8,128)(2,1)} %q_hbm.1, bf16[512,1024]{1,0:T(8,128)(2,1)} %k_hbm.1, bf16[512,1024]{1,0:T(8,128)(2,1)} %v_hbm.1, f32[8,512]{1,0:T(8,128)} %ld.1, bf16[128,4096]{1,0:T(8,128)(2,1)} %res_hbm.1, ...), custom_call_target="tpu_custom_call" | custom-call | tf_op jit(solution)/shard_map/layer/pallas_call | solution.py:583
  94.9 1.9 %copy.11 = bf16[1,1,2,128,1024]{4,3,2,1,0:T(8,128)(2,1)} copy(bf16[1,1,2,128,1024]{4,3,2,1,0:T(8,128)(2,1)} %bitcast.3) | data formatting | bytes 1048576

commit v6 on v5

--- a/solution.py
+++ b/solution.py
@@ -560,20 +560,23 @@
     for m in range(1, NX):
         arrive(tb.at[mod(x - m, NX)], t_r.at[m - 1])
         sent(tb_s, t_s.at[m - 1])
+    def holds(s, p):
+        hit = jnp.logical_and(tb[p, 0] == x, tb[p, 1] == s).astype(F32)
+        return jnp.broadcast_to(hit[0:1, 0:1], (PAGE, KVW)) > 0.5
+
+    for s in range(2):
+        total = jnp.zeros((PAGE, KVW), BF16)
+        for p in (x, x_left, x_right):
+            total = jnp.where(holds(s, p), pg[p], total)
+        cache[s] = total
     for n in range(NT):
         sent(pg.at[0, :, pl.ds(0, TW)], g_s.at[0, n])
         sent(pg.at[0, :, pl.ds(0, TW)], g_s.at[1, n])
         sent(pg.at[0, :, pl.ds(0, TW)], g_f.at[n])
     for n in range(NT):
         arrive(pg.at[x_far, :, tile(n)], g_r.at[2, n])
-    here = [tb[p, 0] == x for p in range(NX)]
     for s in range(2):
-        total = jnp.zeros((PAGE, KVW), BF16)
-        for p in range(NX):
-            hit = jnp.logical_and(here[p], tb[p, 1] == s).astype(F32)
-            hit = jnp.broadcast_to(hit[0:1, 0:1], (PAGE, KVW))
-            total = jnp.where(hit > 0.5, pg[p], total)
-        cache[s] = total
+        cache[s] = jnp.where(holds(s, x_far), pg[x_far], cache[s])
 
 
 def on_device(query_rows, key_rows, value_rows, log_decay, residual, out_weight, norm_gain, kv_weight, block_table):

time: 97 us -> 96.9 us (level)
  no operation moved by 1% of the time
where the time goes in v6:
time: 96.9 us; the launch traced here: 96.7 us
  Pallas kernels  94.8 us (98%)
  local copies, waits for them, and re-layouts  1.87 us (2%)
    pallas_call x1, Pallas kernels, on_device(): pl.pallas_call(kernel, out_shape=jax.ShapeDtypeStruct((2, PAGE, KVW), BF1...  94.8 us

profile of v6, /device:TPU:6, one launch (start us, length us, event | category | flops | bytes accessed | tf_op | source)
XLA Modules:
  0.0 96.7 jit_solution(17370270448430837792)
XLA Ops:
  0.0 94.8 %layer.1 = bf16[2,128,1024]{2,1,0:T(8,128)(2,1)} custom-call(bf16[64,1024]{1,0:T(8,128)(2,1)} %bitcast.4, bf16[64,1024]{1,0:T(8,128)(2,1)} %kw.1, bf16[512,1024]{1,0:T(8,128)(2,1)} %q_hbm.1, bf16[512,1024]{1,0:T(8,128)(2,1)} %k_hbm.1, bf16[512,1024]{1,0:T(8,128)(2,1)} %v_hbm.1, f32[8,512]{1,0:T(8,128)} %ld.1, bf16[128,4096]{1,0:T(8,128)(2,1)} %res_hbm.1, ...), custom_call_target="tpu_custom_call" | custom-call | tf_op jit(solution)/shard_map/layer/pallas_call | solution.py:586
  94.9 1.9 %copy.11 = bf16[1,1,2,128,1024]{4,3,2,1,0:T(8,128)(2,1)} copy(bf16[1,1,2,128,1024]{4,3,2,1,0:T(8,128)(2,1)} %bitcast.3) | data formatting | bytes 1048576

commit v7 on v6

--- a/solution.py
+++ b/solution.py
@@ -229,7 +229,8 @@
     loads[0].wait()
     loads[1].wait()
 
-    def update(h, carry):
+    def update(n, carry):
+        h = lax.rem(n + 4 * (1 - c), HEADS)
         cb = ccol[h]
         gap = jnp.exp(cb[BLK - 1 : BLK, :] - cb)
         weighted = (k_s[:, head_cols(h)].astype(F32) * gap).astype(BF16)
@@ -238,11 +239,12 @@
         )
         return carry
 
-    lax.fori_loop(0, HEADS, update, 0)
-    gather(1, 0)
+    lax.fori_loop(0, 4, update, 0)
     ub_s[...] = u_s[pl.ds(4 * (1 - c), 4)].astype(BF16)
     send(ub_s, ub_r, s1_s.at[0], s1_r.at[0], partner).start()
     send(a_s, a_r, s1_s.at[1], s1_r.at[1], partner).start()
+    lax.fori_loop(4, HEADS, update, 0)
+    gather(1, 0)
 
     def chip_parts():
         own = u_s[pl.ds(4 * c, 4)]

time: 96.9 us -> 96.8 us (level)
  no operation moved by 1% of the time
where the time goes in v7:
time: 96.8 us; the launch traced here: 96.6 us
  Pallas kernels  94.8 us (98%)
  local copies, waits for them, and re-layouts  1.87 us (2%)
    pallas_call x1, Pallas kernels, on_device(): pl.pallas_call(kernel, out_shape=jax.ShapeDtypeStruct((2, PAGE, KVW), BF1...  94.8 us

profile of v7, /device:TPU:6, one launch (start us, length us, event | category | flops | bytes accessed | tf_op | source)
XLA Modules:
  0.0 96.6 jit_solution(4984536805494654573)
XLA Ops:
  0.0 94.8 %layer.1 = bf16[2,128,1024]{2,1,0:T(8,128)(2,1)} custom-call(bf16[64,1024]{1,0:T(8,128)(2,1)} %bitcast.4, bf16[64,1024]{1,0:T(8,128)(2,1)} %kw.1, bf16[512,1024]{1,0:T(8,128)(2,1)} %q_hbm.1, bf16[512,1024]{1,0:T(8,128)(2,1)} %k_hbm.1, bf16[512,1024]{1,0:T(8,128)(2,1)} %v_hbm.1, f32[8,512]{1,0:T(8,128)} %ld.1, bf16[128,4096]{1,0:T(8,128)(2,1)} %res_hbm.1, ...), custom_call_target="tpu_custom_call" | custom-call | tf_op jit(solution)/shard_map/layer/pallas_call | solution.py:588
  94.8 1.9 %copy.11 = bf16[1,1,2,128,1024]{4,3,2,1,0:T(8,128)(2,1)} copy(bf16[1,1,2,128,1024]{4,3,2,1,0:T(8,128)(2,1)} %bitcast.3) | data formatting | bytes 1048576
